TPU v7x, 512 devices: a whole 4x8x8 slice. The times are simulated.
512 devices in a mesh: grid: 128 (over z, x_hi, y), spec: 4 (over x_lo, core).
Axes of the slice: x: 4 (x_hi: 2, x_lo: 2; x = x_hi * 2 + x_lo), y: 8, z: 8, core: 2. Of those that a mesh axis runs over, the one named last changes fastest.
Arguments:
- energy: float32 [36, 36, 512, 128], P('spec', None, 'grid'), may hold values from 0.05 to 1
- nest_energy: float32 [36, 36, 512, 128], P('spec', None, 'grid'), may hold values from 0.05 to 1
- ocean_mask: int32 [512, 128], P('grid'), may hold values 0 or 1
- wind_field: float32 [2, 512, 128], P(None, 'grid'), may hold values from -6 to 6
- rim_cell: int32 [16384, 2], P('grid'), may hold values from 0 to 511, as said below
- rim_dest: int32 [16384, 1], P('grid'), may hold values from 0 to 127; in each aligned block of 128 rows (0 to 127, 128 to 255, ...) at most 2 rows name the same one
- rim_target: int32 [16384], P('grid'), may hold values from 0 to 511
- rim_weight: float32 [16384, 3], P('grid'), may hold values from 0.1 to 0.9
Outputs:
- global_next: float32 [36, 36, 512, 128], P('spec', None, 'grid')
- nest_next: float32 [36, 36, 512, 128], P('spec', None, 'grid')
Inputs may be any that keep to these rules, and one draw needn't show every extreme that they name: `rim_cell`: rows of device g of the grid axis have column 0 between g * 4 and (g + 1) * 4 - 1; column 1 is at most 126. `rim_dest`: the 128 rows of one device name any one nest device at most 2 times, and some device's rows name one exactly 2 times.
All inputs are finite; a program needn't handle non-finite values. No bound on the sum of `ocean_mask` on one device may be relied on, other than what follows from the above.
Results may differ from a plain program's by a relative error of at most 0.003.
Values may be sent and summed in bfloat16 or wider, within the bound.
A program may use at most 64 MiB of HBM per device.

v0:
```python
import jax
import jax.numpy as jnp
from jax import lax
from jax.sharding import PartitionSpec as P

FREQS = 36
ANGLES = 36


ratio_step = 1.1
speed_coef = 0.054
wind_coef = 0.05
dissip_coef = 0.2
nonlin_coef = 0.12
nest_speedup = 2.0
band_reach = 5


def extended_2(x, sides, width, wrap):
    for axis, dim in sides:
        peers, length = (lax.axis_size(axis), x.shape[dim])
        up = [(i, (i + 1) % peers) for i in range(peers if wrap else peers - 1)]
        down = [(j, i) for i, j in up]
        last = lax.slice_in_dim(x, length - width, length, axis=dim)
        leading = lax.slice_in_dim(x, 0, width, axis=dim)
        before = lax.ppermute(last, axis, up)
        after = lax.ppermute(leading, axis, down)
        x = jnp.concatenate([before, x, after], axis=dim)
    return x


def passed_along(block, axis, distance):
    devices = range(lax.axis_size(axis))
    route = [((i - distance) % len(devices), i) for i in devices]
    return lax.ppermute(block, axis, route)


def freq_ratio(first_band, band_count):
    band_ranks = jnp.asarray(first_band).astype(jnp.float32) + jnp.arange(band_count).astype(
        jnp.float32
    )
    return jnp.power(jnp.float32(ratio_step), band_ranks - FREQS // 2)


def lat_secant(lat_rows):
    lat_degrees = -60.0 + 120.0 * (jnp.arange(lat_rows).astype(jnp.float32) + 0.5) / lat_rows
    return 1.0 / jnp.cos(lat_degrees * (jnp.pi / 180.0))


def headings():
    return 2.0 * jnp.pi * jnp.arange(ANGLES).astype(jnp.float32) / ANGLES


def courant_pair(ratios, lat_scale, speedup):
    group_speed = speedup * speed_coef / ratios
    heading = headings()
    along_lon = (
        group_speed[:, None, None, None]
        * jnp.cos(heading)[None, :, None, None]
        * lat_scale[None, None, None, :]
    )
    along_lat = group_speed[:, None, None, None] * jnp.sin(heading)[None, :, None, None]
    return (along_lon, along_lat)


def advect(padded, along_lon, along_lat):
    center = padded[:, :, 1:-1]
    west_cells = padded[:, :, :-2]
    east_cells = padded[:, :, 2:]
    zeros_row = jnp.zeros_like(center[..., :1])
    south_cells = jnp.concatenate([zeros_row, center[..., :-1]], axis=3)
    north_cells = jnp.concatenate([center[..., 1:], zeros_row], axis=3)
    flux_lon = jnp.maximum(along_lon, 0.0) * (center - west_cells) + jnp.minimum(along_lon, 0.0) * (
        east_cells - center
    )
    flux_lat = jnp.maximum(along_lat, 0.0) * (center - south_cells) + jnp.minimum(
        along_lat, 0.0
    ) * (north_cells - center)
    return center - flux_lon - flux_lat


def nonlinear(banded, ratios_padded):
    band_count = banded.shape[0] - 2 * band_reach
    centre = banded[3 : band_count + 8]
    strength = nonlin_coef * ratios_padded[3 : band_count + 8][:, None, None, None]
    result = jnp.zeros_like(banded[band_reach : band_reach + band_count])
    for mirror in (1, -1):
        upper_pair = jnp.roll(banded[5 : band_count + 10], -3 * mirror, axis=1)
        lower_pair = jnp.roll(banded[0 : band_count + 5], mirror, axis=1)
        transfer = strength * (
            centre * centre * (upper_pair + lower_pair) - 2.0 * centre * upper_pair * lower_pair
        )
        result = (
            result
            - 2.0 * transfer[2 : band_count + 2]
            + jnp.roll(transfer[0:band_count], 3 * mirror, axis=1)
            + jnp.roll(transfer[5 : band_count + 5], -mirror, axis=1)
        )
    return result


def step_sources(advected, banded, ratios, ratios_padded, wind_block, mean_energy):
    heading = headings()
    along_wind = jnp.maximum(
        wind_block[0][None, None] * jnp.cos(heading)[None, :, None, None]
        + wind_block[1][None, None] * jnp.sin(heading)[None, :, None, None],
        0.0,
    )
    wind_gain = wind_coef * ratios[:, None, None, None] * along_wind * advected
    transfer = nonlinear(banded, ratios_padded)
    return (advected + wind_gain + transfer) / (
        1.0 + dissip_coef * (ratios * ratios)[:, None, None, None] * mean_energy[None, None]
    )


def interpolate(spectra_flat, base_cell, east_cell, rim_weight):
    east_share = rim_weight[:, 0]
    north_share = rim_weight[:, 1]
    corner_sw = jnp.take(spectra_flat, base_cell, axis=1)
    corner_nw = jnp.take(spectra_flat, base_cell + 1, axis=1)
    corner_se = jnp.take(spectra_flat, east_cell, axis=1)
    corner_ne = jnp.take(spectra_flat, east_cell + 1, axis=1)
    mixed = (1.0 - east_share) * (1.0 - north_share) * corner_sw + (
        1.0 - east_share
    ) * north_share * corner_nw
    mixed = (
        mixed + east_share * (1.0 - north_share) * corner_se + east_share * north_share * corner_ne
    )
    return mixed.astype(jnp.bfloat16)


def blend(totals, nest_flat, spectra, targets, weights):
    picked = jnp.take(nest_flat, targets, axis=1)
    return totals.at[:, targets].add(weights[None, :] * (spectra.astype(jnp.float32) - picked))


def per_device(
    energy, nest_energy, ocean_mask, wind_field, rim_cell, rim_dest, rim_target, rim_weight
):
    grid_rank = lax.axis_index("grid")
    grid_count = lax.axis_size("grid")
    quarter_count = grid_count // 4
    bands_dev = energy.shape[0]
    lon_dev = energy.shape[2]
    lat_rows = energy.shape[3]
    bin_count = bands_dev * ANGLES
    first_band = lax.axis_index("spec") * bands_dev
    ratios = freq_ratio(first_band, bands_dev)
    global_padded = extended_2(energy, (("grid", 2),), 1, True)
    nest_padded = extended_2(nest_energy, (("grid", 2),), 1, True)
    lower_keep = jnp.logical_and(grid_rank != quarter_count, grid_rank != 3 * quarter_count)
    upper_keep = jnp.logical_and(grid_rank != quarter_count - 1, grid_rank != 3 * quarter_count - 1)
    nest_padded = jnp.concatenate(
        [
            nest_padded[:, :, :1] * lower_keep.astype(jnp.float32),
            nest_padded[:, :, 1:-1],
            nest_padded[:, :, -1:] * upper_keep.astype(jnp.float32),
        ],
        axis=2,
    )
    along_lon, along_lat = courant_pair(ratios, lat_secant(lat_rows), 1.0)
    advected = advect(global_padded, along_lon, along_lat) * ocean_mask.astype(jnp.float32)
    band_weight = 0.1 * ratios
    partial_value = jnp.sum(band_weight[:, None, None, None] * advected, axis=(0, 1))
    total_energy = lax.psum(partial_value, "spec")
    mean_energy = total_energy / (ANGLES * (0.1 * jnp.sum(freq_ratio(0, FREQS))))
    banded = extended_2(advected, (("spec", 0),), band_reach, False)
    ratios_padded = freq_ratio(first_band - band_reach, bands_dev + 2 * band_reach)
    global_next = step_sources(advected, banded, ratios, ratios_padded, wind_field, mean_energy)
    east_column = passed_along(global_next[:, :, :1], "grid", -1)
    extended = jnp.concatenate([global_next, east_column], axis=2).reshape(
        bin_count, (lon_dev + 1) * lat_rows
    )
    local_col = rim_cell[:, 0] - grid_rank * lon_dev
    base_cell = local_col * lat_rows + rim_cell[:, 1]
    east_cell = base_cell + lat_rows
    boundary = interpolate(extended, base_cell, east_cell, rim_weight)
    nest_lon, nest_lat = courant_pair(ratios, jnp.ones((lat_rows,), jnp.float32), nest_speedup)
    nest_flat = advect(nest_padded, nest_lon, nest_lat).reshape(bin_count, lon_dev * lat_rows)
    dest_rows = rim_dest[:, 0]
    relax_rate = rim_weight[:, 2]
    spectra = lax.all_gather(boundary, "grid", axis=1, tiled=True)
    dests = lax.all_gather(dest_rows[None, :], "grid", axis=1, tiled=True)
    targets = lax.all_gather(rim_target[None, :], "grid", axis=1, tiled=True)
    relaxes = lax.all_gather(
        relax_rate[None, :].astype(jnp.bfloat16), "grid", axis=1, tiled=True
    ).astype(jnp.float32)
    weights = jnp.where(dests[0] == grid_rank, relaxes[0], 0.0)
    increments = blend(jnp.zeros_like(nest_flat), nest_flat, spectra, targets[0], weights)
    nest_next = (nest_flat + increments).reshape(bands_dev, ANGLES, lon_dev, lat_rows)
    return (global_next, nest_next)


def solution(mesh):
    in_specs = (
        P("spec", None, "grid", None),
        P("spec", None, "grid", None),
        P("grid", None),
        P(None, "grid", None),
        P("grid", None),
        P("grid", None),
        P("grid"),
        P("grid", None),
    )
    out_specs = (P("spec", None, "grid", None), P("spec", None, "grid", None))
    return jax.shard_map(
        per_device, mesh=mesh, in_specs=in_specs, out_specs=out_specs, check_vma=False
    )
```

profile of v0, /device:TPU:2, one launch (start us, length us, event | category | flops | bytes accessed | tf_op | source)
XLA Modules:
  0.0 1304.8 jit_solution(18204912658880549547)
XLA Ops:
  7.2 1.2 copy.26
  8.4 3.5 collective-permute-start
  11.9 13.9 %collective-permute-start.1 = (f32[9,36,1,128]{3,1,2,0:T(8,128)S(1)}, f32[9,36,1,128]{3,1,2,0:T(8,128)}, u32[]{:S(2)}, u32[]{:S(2)}) collective-permute-start(f32[9,36,1,128]{3,1,2,0:T(8,128)S(1)} %get-tuple-element.26), channel_id=1, source_target_pairs={{4,0},{8,4},{12,8},{16,12},{20,16},{24,20},{28,24},{32,28},{36,32}... | collective-permute-start | bytes 497672 | tf_op jit(solution)/shard_map/ppermute | solution.py:27
  26.0 0.3 fusion.54
  26.3 0.3 copy-done.2
  26.7 0.1 add_maximum_fusion
  26.8 0.1 multiply_maximum_fusion
  27.0 0.6 power_reduce_fusion
  28.3 0.2 collective-permute-done
  28.5 1.1 collective-permute-done.1
  29.6 1.6 multiply_reduce_fusion
  31.2 5.7 psum.7
  37.0 1.9 collective-permute-start.2
  38.9 3.6 collective-permute-start.3
  42.6 0.1 multiply_add_fusion.1
  42.7 5.4 collective-permute-done.3
  48.1 0.1 fusion.11
  48.2 0.2 fusion.10
  48.4 0.8 subtract_multiply_fusion.1
  49.6 0.7 fusion.17
  50.3 10.2 collective-permute-start.6
  60.6 3.0 collective-permute-done.6
  63.7 0.2 copy.35
  63.9 0.1 pad.66
  64.0 0.2 copy.47
  64.2 0.3 copy.36
  64.5 0.8 gather_fusion.3
  65.3 0.8 gather_fusion.2
  66.1 0.8 gather_fusion.1
  66.9 0.8 gather_fusion
  67.6 0.9 fusion.40
  68.5 0.3 fusion.56
  68.8 10.1 collective-permute-start.5
  79.0 1.9 collective-permute-start.4
  80.9 355.6 %all-gather.2 = bf16[16384,1]{0,1:T(2,128)(2,1)S(1)} all-gather(bf16[128,1]{0,1:T(2,128)(2,1)S(1)} %slice.203), channel_id=4, replica_groups=mesh['grid'=128,'spec'=4] {'grid'}, dimensions={0}, use_global_device_ids=true | all-gather | bytes 33024 | tf_op jit(solution)/shard_map/all_gather | solution.py:185
  436.5 347.4 %all-gather.3 = s32[128,1,128]{2,1,0:T(1,128)S(1)} all-gather(s32[1,1,128]{2,1,0:T(1,128)S(1)} %bitcast.95), channel_id=2, replica_groups=mesh['grid'=128,'spec'=4] {'grid'}, dimensions={0}, use_global_device_ids=true | all-gather | bytes 66048 | tf_op jit(solution)/shard_map/all_gather | solution.py:184
  783.9 349.4 %all-gather.1 = s32[16384,1]{0,1:T(1,128)S(1)} all-gather(s32[128,1]{0,1:T(1,128)S(1)} %copy-done.7), channel_id=3, replica_groups=mesh['grid'=128,'spec'=4] {'grid'}, dimensions={0}, use_global_device_ids=true | all-gather | bytes 66048 | tf_op jit(solution)/shard_map/all_gather | solution.py:183
  1133.5 0.1 compare_select_fusion.1
  1133.6 0.4 fusion.55
  1134.0 0.2 copy.34
  1134.2 0.2 copy.32
  1134.4 2.1 fusion.36
  1136.5 0.1 pad.65
  1136.7 0.3 copy.41
  1136.9 1.0 copy.43
  1138.0 158.7 %scatter_custom_fusion = f32[324,512]{0,1:T(8,128)S(1)} fusion(f32[324,512]{0,1:T(8,128)S(1)} %copy.41, s32[16384]{0:T(1024)S(1)} %bitcast.94, bf16[324,16384]{0,1:T(8,128)(2,1)} %all-gather.6.cloned.1.call-done, f32[]{:T(128)} %constant.40.clone.1, f32[16384]{0:T(1024)S(1)} %bitcast.92, pred[16384]{0:T(1024)(128)(4,1)S(1)} %compare_and_fusion, ...), kind=kCustom, calls=%fused_computation.6 | custom fusion | flops 26542080 | bytes 12214276 | tf_op jit(solution)/shard_map/scatter-add | solution.py:134
  1296.6 0.2 copy.42
  1296.9 1.1 reshape.362
  (62 shorter events, 1.2 us)
Async XLA Ops:
  7.2 18.7 %copy-start.5 = (s32[128,2]{0,1:T(2,128)S(1)}, s32[128,2]{0,1:T(2,128)}, u32[]{:S(2)}) copy-start(s32[128,2]{0,1:T(2,128)} %param.14) | copy-start | bytes 3076
  7.2 1130.8 %all-gather.6.cloned.1.call-start = ((), (), s32[]{:S(2)}) async-start(), calls=%async_computation | async-start | bytes 12681216 | tf_op jit(solution)/shard_map/all_gather | solution.py:182
  8.4 20.1 %collective-permute-start = (f32[9,36,1,128]{3,1,2,0:T(8,128)S(1)}, f32[9,36,1,128]{3,1,2,0:T(8,128)S(1)}, u32[]{:S(2)}, u32[]{:S(2)}) collective-permute-start(f32[9,36,1,128]{3,1,2,0:T(8,128)S(1)} %get-tuple-element.25), channel_id=1, source_target_pairs={{0,4},{4,8},{8,12},{12,16},{16,20},{20,24},{24,28},{28,32},{32,36}... | collective-permute-start | bytes 497672 | tf_op jit(solution)/shard_map/ppermute | solution.py:26
  11.9 17.7 %collective-permute-start.1 = (f32[9,36,1,128]{3,1,2,0:T(8,128)S(1)}, f32[9,36,1,128]{3,1,2,0:T(8,128)}, u32[]{:S(2)}, u32[]{:S(2)}) collective-permute-start(f32[9,36,1,128]{3,1,2,0:T(8,128)S(1)} %get-tuple-element.26), channel_id=1, source_target_pairs={{4,0},{8,4},{12,8},{16,12},{20,16},{24,20},{28,24},{32,28},{36,32}... | collective-permute-start | bytes 497672 | tf_op jit(solution)/shard_map/ppermute | solution.py:27
  26.0 0.7 copy-start.2
  26.0 0.7 copy-start.3
  26.0 1.0 copy-start.4
  28.5 1.1 copy-start.1
  37.0 11.2 collective-permute-start.2
  38.9 9.1 collective-permute-start.3
  50.3 13.3 %collective-permute-start.6 = (f32[9,36,1,128]{3,1,2,0:T(8,128)S(1)}, f32[9,36,1,128]{3,1,2,0:T(8,128)S(1)}, u32[]{:S(2)}, u32[]{:S(2)}) collective-permute-start(f32[9,36,1,128]{3,1,2,0:T(8,128)S(1)} %slice.245), channel_id=1, source_target_pairs={{4,0},{8,4},{12,8},{16,12},{20,16},{24,20},{28,24},{32,28},{36,32}... | collective-permute-start | bytes 497672 | tf_op jit(solution)/shard_map/ppermute | solution.py:35
  66.8 1.7 copy-start
  67.6 368.9 %copy-start.6 = (s32[128]{0:T(128)S(1)}, s32[128]{0:T(128)}, u32[]{:S(2)}) copy-start(s32[128]{0:T(128)} %param.16) | copy-start | bytes 1540
  67.6 716.3 %copy-start.7 = (s32[128,1]{0,1:T(1,128)S(1)}, s32[128,1]{0,1:T(1,128)}, u32[]{:S(2)}) copy-start(s32[128,1]{0,1:T(1,128)} %param.15) | copy-start | bytes 1540
  68.8 1065.2 %collective-permute-start.5 = (f32[9,36,1,128]{3,1,2,0:T(8,128)S(1)}, f32[9,36,1,128]{3,1,2,0:T(8,128)S(1)}, u32[]{:S(2)}, u32[]{:S(2)}) collective-permute-start(f32[9,36,1,128]{3,1,2,0:T(8,128)S(1)} %copy.45), channel_id=1, source_target_pairs={{4,0},{8,4},{12,8},{16,12},{20,16},{24,20},{28,24},{32,28},{36,32}... | collective-permute-start | bytes 497672 | tf_op jit(solution)/shard_map/ppermute | solution.py:27
  79.0 1055.2 %collective-permute-start.4 = (f32[9,36,1,128]{3,1,2,0:T(8,128)S(1)}, f32[9,36,1,128]{3,1,2,0:T(8,128)S(1)}, u32[]{:S(2)}, u32[]{:S(2)}) collective-permute-start(f32[9,36,1,128]{3,1,2,0:T(8,128)S(1)} %copy.44), channel_id=1, source_target_pairs={{0,4},{4,8},{8,12},{12,16},{16,20},{20,24},{24,28},{28,32},{32,36}... | collective-permute-start | bytes 497672 | tf_op jit(solution)/shard_map/ppermute | solution.py:26
Sparse Core Ops, SparseCore 0:
  68.6 180.2 all-gather.5
where the time goes:
time: 1310 us; the launch traced here: 1300 us
  blocking collectives  1060 us (81%)
  other arithmetic  167 us (13%)
  starting transfers between devices  45.2 us (3%)
  between operations  15.3 us (1%)
    all_gather x1, blocking collectives, per_device(): lax.all_gather(relax_rate[None, :].astype(jnp.bfloat16), 'grid', axis=1,...  356 us
    all_gather x1, blocking collectives, per_device(): dests = lax.all_gather(dest_rows[None, :], 'grid', axis=1, tiled=True)  349 us
    all_gather x1, blocking collectives, per_device(): targets = lax.all_gather(rim_target[None, :], 'grid', axis=1, tiled=True)  347 us
    scatter-add x1, other arithmetic, blend(): totals.at[:, targets]  159 us
    ppermute x3, starting transfers between devices, extended_2(): after = lax.ppermute(leading, axis, down)  27.6 us
  transfers between devices with their start and end apart: 8, of which 4 were waited for; matrix products, arithmetic and copies ran while one was open for 0% of the time, Pallas kernels for 0%

commit v1 on v0

--- a/solution.py
+++ b/solution.py
@@ -1,6 +1,10 @@
+import functools
+
 import jax
 import jax.numpy as jnp
 from jax import lax
+from jax.experimental import pallas as pl
+from jax.experimental.pallas import tpu as pltpu
 from jax.sharding import PartitionSpec as P
 
 FREQS = 36
@@ -14,6 +18,8 @@
 nonlin_coef = 0.12
 nest_speedup = 2.0
 band_reach = 5
+SLOTS = 2
+MESH = pl.DeviceIdType.MESH
 
 
 def extended_2(x, sides, width, wrap):
@@ -113,25 +119,56 @@
     )
 
 
-def interpolate(spectra_flat, base_cell, east_cell, rim_weight):
-    east_share = rim_weight[:, 0]
-    north_share = rim_weight[:, 1]
-    corner_sw = jnp.take(spectra_flat, base_cell, axis=1)
-    corner_nw = jnp.take(spectra_flat, base_cell + 1, axis=1)
-    corner_se = jnp.take(spectra_flat, east_cell, axis=1)
-    corner_ne = jnp.take(spectra_flat, east_cell + 1, axis=1)
-    mixed = (1.0 - east_share) * (1.0 - north_share) * corner_sw + (
-        1.0 - east_share
-    ) * north_share * corner_nw
-    mixed = (
-        mixed + east_share * (1.0 - north_share) * corner_se + east_share * north_share * corner_ne
-    )
-    return mixed.astype(jnp.bfloat16)
-
-
-def blend(totals, nest_flat, spectra, targets, weights):
-    picked = jnp.take(nest_flat, targets, axis=1)
-    return totals.at[:, targets].add(weights[None, :] * (spectra.astype(jnp.float32) - picked))
+def exchange_kernel(count, send_ref, recv_ref, send_sem, recv_sem):
+    me = lax.axis_index("grid")
+    barrier = pltpu.get_barrier_semaphore()
+
+    def peer(i):
+        return lax.rem(me + i, count)
+
+    def greet(i, carry):
+        pl.semaphore_signal(barrier, inc=1, device_id={"grid": peer(i)}, device_id_type=MESH)
+        return carry
+
+    lax.fori_loop(1, count, greet, 0)
+    pl.semaphore_wait(barrier, count - 1)
+    own = pltpu.make_async_copy(send_ref.at[me], recv_ref.at[me], recv_sem)
+    own.start()
+
+    def post(i, carry):
+        dest = peer(i)
+        pltpu.make_async_remote_copy(
+            src_ref=send_ref.at[dest],
+            dst_ref=recv_ref.at[me],
+            send_sem=send_sem,
+            recv_sem=recv_sem,
+            device_id={"grid": dest},
+            device_id_type=MESH,
+        ).start()
+        return carry
+
+    lax.fori_loop(1, count, post, 0)
+    others = send_ref.at[pl.ds(0, count - 1)]
+    pltpu.make_async_copy(others, others, send_sem).wait()
+    pltpu.make_async_copy(recv_ref, recv_ref, recv_sem).wait()
+
+
+def exchange(blocks):
+    count = blocks.shape[0]
+    return pl.pallas_call(
+        functools.partial(exchange_kernel, count),
+        out_shape=jax.ShapeDtypeStruct(blocks.shape, blocks.dtype),
+        in_specs=[pl.BlockSpec(memory_space=pltpu.VMEM)],
+        out_specs=pl.BlockSpec(memory_space=pltpu.VMEM),
+        scratch_shapes=[pltpu.SemaphoreType.DMA, pltpu.SemaphoreType.DMA],
+        compiler_params=pltpu.CompilerParams(collective_id=0, has_side_effects=True),
+        name="rim_exchange",
+    )(blocks)
+
+
+def split_16(x):
+    high = lax.reduce_precision(x, 8, 7)
+    return high, x - high
 
 
 def per_device(
@@ -172,22 +209,72 @@
         bin_count, (lon_dev + 1) * lat_rows
     )
     local_col = rim_cell[:, 0] - grid_rank * lon_dev
-    base_cell = local_col * lat_rows + rim_cell[:, 1]
-    east_cell = base_cell + lat_rows
-    boundary = interpolate(extended, base_cell, east_cell, rim_weight)
+    cols = jnp.arange(lon_dev + 1)[None, :]
+    rows = jnp.arange(lat_rows)[None, :]
+    ex = rim_weight[:, 0:1]
+    ny = rim_weight[:, 1:2]
+    col_share = jnp.where(cols == local_col[:, None], 1.0 - ex, 0.0) + jnp.where(
+        cols == local_col[:, None] + 1, ex, 0.0
+    )
+    row_share = jnp.where(rows == rim_cell[:, 1:2], 1.0 - ny, 0.0) + jnp.where(
+        rows == rim_cell[:, 1:2] + 1, ny, 0.0
+    )
+    corners = (col_share[:, :, None] * row_share[:, None, :]).reshape(rim_cell.shape[0], -1)
+    boundary = lax.dot_general(
+        corners, extended, (((1,), (1,)), ((), ())), precision=lax.Precision.HIGHEST
+    )
+    dest = rim_dest[:, 0]
+    points = dest.shape[0]
+    order = jnp.arange(points)
+    earlier = (dest[:, None] == dest[None, :]) & (order[None, :] < order[:, None])
+    slot = jnp.sum(earlier.astype(jnp.int32), axis=1)
+    relax_high, relax_low = split_16(rim_weight[:, 2:3])
+    target = rim_target[:, None]
+    lanes = 128
+    width = -(-(bin_count + 4) // lanes) * lanes
+    payload = jnp.concatenate(
+        [
+            boundary,
+            (target // lat_rows).astype(jnp.float32),
+            (target % lat_rows).astype(jnp.float32),
+            relax_high,
+            relax_low,
+            jnp.zeros((points, width - bin_count - 4), jnp.float32),
+        ],
+        axis=1,
+    ).astype(jnp.bfloat16)
+    slot_ids = jnp.arange(SLOTS)[:, None, None]
+    names = jnp.arange(grid_count)[None, :, None]
+    chosen = ((slot[None, None, :] == slot_ids) & (dest[None, None, :] == names)).astype(
+        jnp.bfloat16
+    )
+    packed = lax.dot_general(
+        chosen, payload, (((2,), (0,)), ((), ())), preferred_element_type=jnp.float32
+    ).astype(jnp.bfloat16)
+    per_slot = width // lanes
+    blocks = jnp.transpose(packed.reshape(SLOTS, grid_count, per_slot, lanes), (1, 0, 2, 3))
+    blocks = blocks.reshape(grid_count, SLOTS * per_slot, lanes)
+    blocks = jnp.pad(blocks, ((0, 0), (0, 8 - SLOTS * per_slot), (0, 0)))
+    arrived = exchange(blocks)
     nest_lon, nest_lat = courant_pair(ratios, jnp.ones((lat_rows,), jnp.float32), nest_speedup)
     nest_flat = advect(nest_padded, nest_lon, nest_lat).reshape(bin_count, lon_dev * lat_rows)
-    dest_rows = rim_dest[:, 0]
-    relax_rate = rim_weight[:, 2]
-    spectra = lax.all_gather(boundary, "grid", axis=1, tiled=True)
-    dests = lax.all_gather(dest_rows[None, :], "grid", axis=1, tiled=True)
-    targets = lax.all_gather(rim_target[None, :], "grid", axis=1, tiled=True)
-    relaxes = lax.all_gather(
-        relax_rate[None, :].astype(jnp.bfloat16), "grid", axis=1, tiled=True
-    ).astype(jnp.float32)
-    weights = jnp.where(dests[0] == grid_rank, relaxes[0], 0.0)
-    increments = blend(jnp.zeros_like(nest_flat), nest_flat, spectra, targets[0], weights)
-    nest_next = (nest_flat + increments).reshape(bands_dev, ANGLES, lon_dev, lat_rows)
+    arrived = arrived[:, : SLOTS * per_slot].reshape(grid_count * SLOTS, width)
+    facts = arrived[:, bin_count : bin_count + 4].astype(jnp.float32)
+    cell = facts[:, 0:1] * lat_rows + facts[:, 1:2]
+    hit = cell == jnp.arange(lon_dev * lat_rows)[None, :].astype(jnp.float32)
+    share_high = jnp.where(hit, facts[:, 2:3], 0.0)
+    share_low = jnp.where(hit, facts[:, 3:4], 0.0)
+    total_share = jnp.sum(share_high + share_low, axis=0)
+    spectra = arrived[:, :bin_count]
+    gained = lax.dot_general(
+        jnp.concatenate([spectra, spectra], axis=0),
+        jnp.concatenate([share_high, share_low], axis=0).astype(jnp.bfloat16),
+        (((0,), (0,)), ((), ())),
+        preferred_element_type=jnp.float32,
+    )
+    nest_next = (nest_flat * (1.0 - total_share)[None, :] + gained).reshape(
+        bands_dev, ANGLES, lon_dev, lat_rows
+    )
     return (global_next, nest_next)
 
 

time: 1310 us -> 113 us (0.09)
  the two profiles are of different devices: /device:TPU:2 before, /device:TPU:1 now
where the time goes in v1:
time: 113 us
  starting transfers between devices  37.5 us (33%)
  other arithmetic  27 us (24%)
  Pallas kernels  19.2 us (17%)
  local copies, waits for them, and re-layouts  15.8 us (14%)
  blocking collectives  8.45 us (7%)
  between operations  1.88 us (2%)
  matrix products  1.52 us (1%)
  waiting for transfers between devices  1.23 us (1%)
    ppermute x3, starting transfers between devices, extended_2(): after = lax.ppermute(leading, axis, down)  25.7 us
    pallas_call x1, Pallas kernels, exchange(): pl.pallas_call(functools.partial(exchange_kernel, count), out_shape=jax.S...  19.2 us
    ppermute x3, starting transfers between devices, extended_2(): before = lax.ppermute(last, axis, up)  9.54 us
    psum x1, blocking collectives, per_device(): total_energy = lax.psum(partial_value, 'spec')  8.45 us
    unnamed x50, local copies, waits for them, and re-layouts  6.65 us
    max x2, other arithmetic, advect(): jnp.maximum(along_lon, 0.0) * (center - west_cells)  2.92 us
    reduce_sum x1, other arithmetic, per_device(): jnp.sum(band_weight[:, None, None, None] * advected, axis=(0, 1))  2.52 us
    slice x2, local copies, waits for them, and re-layouts, advect(): south_cells = jnp.concatenate([zeros_row, center[..., :-1]], axis=3)  2.38 us
  transfers between devices with their start and end apart: 7, of which 1 were waited for; matrix products, arithmetic and copies ran while one was open for 29% of the time, Pallas kernels for 0%

profile of v1, /device:TPU:1, one launch (start us, length us, event | category | flops | bytes accessed | tf_op | source)
XLA Modules:
  0.0 112.6 jit_solution(12254265621628816609)
XLA Ops:
  0.6 1.2 %copy.49 = f32[9,36,4,128]{3,1,2,0:T(8,128)S(1)} copy(f32[9,36,4,128]{3,2,1,0:T(4,128)} %param.8) | data formatting | bytes 1327104 | tf_op args[0]
  1.9 4.0 %collective-permute-start = (f32[9,36,1,128]{3,1,2,0:T(8,128)S(1)}, f32[9,36,1,128]{3,1,2,0:T(8,128)S(1)}, u32[]{:S(2)}, u32[]{:S(2)}) collective-permute-start(f32[9,36,1,128]{3,1,2,0:T(8,128)S(1)} %get-tuple-element.19), channel_id=1, source_target_pairs={{0,4},{4,8},{8,12},{12,16},{16,20},{20,24},{24,28},{28,32},{32,36}... | collective-permute-start | bytes 497672 | tf_op jit(solution)/shard_map/ppermute | solution.py:32
  5.9 14.7 %collective-permute-start.1 = (f32[9,36,1,128]{3,1,2,0:T(8,128)S(1)}, f32[9,36,1,128]{3,1,2,0:T(8,128)S(1)}, u32[]{:S(2)}, u32[]{:S(2)}) collective-permute-start(f32[9,36,1,128]{3,1,2,0:T(8,128)S(1)} %get-tuple-element.20), channel_id=1, source_target_pairs={{4,0},{8,4},{12,8},{16,12},{20,16},{24,20},{28,24},{32,28},{36,32}... | collective-permute-start | bytes 497672 | tf_op jit(solution)/shard_map/ppermute | solution.py:33
  21.0 0.7 copy.68
  21.7 1.9 %collective-permute-start.4 = (f32[9,36,1,128]{3,1,2,0:T(8,128)}, f32[9,36,1,128]{3,1,2,0:T(8,128)}, u32[]{:S(2)}, u32[]{:S(2)}) collective-permute-start(f32[9,36,1,128]{3,1,2,0:T(8,128)} %copy.68), channel_id=1, source_target_pairs={{0,4},{4,8},{8,12},{12,16},{16,20},{20,24},{24,28},{28,32},{32,36}... | collective-permute-start | bytes 497672 | tf_op jit(solution)/shard_map/ppermute | solution.py:32
  23.6 0.7 copy.69
  24.2 9.1 %collective-permute-start.5 = (f32[9,36,1,128]{3,1,2,0:T(8,128)}, f32[9,36,1,128]{3,1,2,0:T(8,128)}, u32[]{:S(2)}, u32[]{:S(2)}) collective-permute-start(f32[9,36,1,128]{3,1,2,0:T(8,128)} %copy.69), channel_id=1, source_target_pairs={{4,0},{8,4},{12,8},{16,12},{20,16},{24,20},{28,24},{32,28},{36,32}... | collective-permute-start | bytes 497672 | tf_op jit(solution)/shard_map/ppermute | solution.py:33
  33.9 0.6 cosine_divide_fusion
  34.6 1.1 %fusion.59 = (f32[9,36,4,127]{3,1,2,0:T(8,128)S(1)}, f32[9,36,4,127]{3,1,2,0:T(8,128)}) fusion(f32[9,36,4,128]{3,1,2,0:T(8,128)S(1)} %copy.49), kind=kLoop, calls=%fused_computation.152 | loop fusion | bytes 2633472 | tf_op jit(solution)/shard_map/slice | solution.py:77
  35.7 0.6 broadcast_multiply_fusion.4
  36.3 0.6 multiply_multiply_fusion
  36.9 0.7 convert_reduce_fusion
  37.6 1.2 %fusion.60 = (f32[9,36,4,127]{3,2,1,0:T(4,128)S(1)}, f32[9,36,4,127]{3,2,1,0:T(4,128)}) fusion(f32[9,36,4,128]{3,2,1,0:T(4,128)S(1)} %copy-done), kind=kLoop, calls=%fused_computation.153 | loop fusion | bytes 2633472 | tf_op jit(solution)/shard_map/slice | solution.py:77
  38.9 0.6 slice_multiply_fusion.3
  39.5 1.3 %slice_bitcast_fusion.1 = (f32[4,128]{1,0:T(4,128)}, f32[4,128]{1,0:T(4,128)}) fusion(f32[2,4,128]{2,1,0:T(4,128)} %param.11), kind=kLoop, calls=%fused_computation.109 | loop fusion | bytes 8192 | tf_op jit(solution)/shard_map/mul | solution.py:111
  40.8 1.4 %fusion.46 = (bf16[128,1]{0,1:T(2,128)(2,1)}, f32[128]{0:T(128)}, f32[128]{0:T(128)}, f32[128]{0:T(128)}, bf16[128,1]{0,1:T(2,128)(2,1)}, /*index=5*/f32[128]{0:T(128)}) fusion(f32[128,3]{0,1:T(4,128)} %param.15), kind=kLoop, calls=%fused_computation.120 | loop fusion | flops 768 | bytes 4096 | tf_op jit(solution)/shard_map/convert.6
  42.2 1.3 %fusion.49 = (bf16[128,1]{0,1:T(2,128)(2,1)}, bf16[128,1]{0,1:T(2,128)(2,1)}) fusion(s32[128]{0:T(128)} %param.14), kind=kLoop, calls=%fused_computation.123 | loop fusion | flops 2944 | bytes 1024 | tf_op jit(solution)/shard_map/convert_element_type | solution.py:239
  43.4 1.1 %iota_compare_fusion.6 = pred[2,128]{1,0:T(4,128)(4,1)} fusion(s32[128]{0:T(128)} %convert_reduce_fusion), kind=kLoop, calls=%fused_computation.115 | loop fusion | flops 256 | bytes 768 | tf_op jit(solution)/shard_map/eq | solution.py:248
  44.6 1.4 %multiply_maximum_fusion.2 = (f32[9,36]{1,0:T(8,128)}, f32[9,36]{1,0:T(8,128)}, f32[9,36]{1,0:T(8,128)S(1)}, f32[9,36]{1,0:T(8,128)}, f32[9,36]{1,0:T(8,128)}, /*index=5*/f32[9,36]{1,0:T(8,128)}, f32[9,36]{1,0:T(8,128)}) fusion(f32[9]{0:T(128)} %get-tuple-element.58, f32[36]{0:T(128)} %get-tuple-element.61, f32[9]{0:T(128)} %get-tuple-element.59, ...), kind=kLoop, calls=%fused_computation.100 | loop fusion | flops 3240 | bytes 9432 | tf_op jit(solution)/shard_map/max | solution.py:79
  45.9 1.5 %multiply_maximum_fusion = (f32[9,36,128]{2,1,0:T(8,128)}, f32[9,36,128]{2,1,0:T(8,128)}) fusion(f32[128]{0:T(128)} %cosine_divide_fusion, f32[9,36]{1,0:T(8,128)S(1)} %get-tuple-element.51), kind=kLoop, calls=%fused_computation.72 | loop fusion | flops 124416 | bytes 333584 | tf_op jit(solution)/shard_map/max | solution.py:79
  47.5 1.4 %add_maximum_fusion = f32[36,4,128]{2,0,1:T(8,128)} fusion(f32[36]{0:T(128)} %get-tuple-element.60, f32[4,128]{1,0:T(4,128)} %get-tuple-element.30, f32[36]{0:T(128)} %get-tuple-element.61, f32[4,128]{1,0:T(4,128)} %get-tuple-element.29), kind=kLoop, calls=%fused_computation.85 | loop fusion | flops 73728 | bytes 78112 | tf_op jit(solution)/shard_map/max | solution.py:110
  48.9 0.8 fusion.55
  49.6 0.7 select_add_fusion.1
  50.3 0.7 select_add_fusion.2
  51.0 0.8 broadcast_multiply_fusion
  52.3 1.3 %convert_element_type.104 = f32[4,128]{1,0:T(4,128)} convert(s32[4,128]{1,0:T(4,128)} %param.10) | non-fusion elementwise | flops 512 | bytes 4096 | tf_op jit(solution)/shard_map/convert_element_type | solution.py:199
  53.5 0.6 power_reduce_fusion
  55.4 0.7 copy-done.4
  56.1 2.5 %multiply_reduce_fusion = (f32[4,128]{1,0:T(4,128)}, f32[9,36,4,128]{3,1,2,0:T(8,128)S(1)}) fusion(f32[9]{0:T(128)} %broadcast_multiply_fusion.5, f32[4,128]{1,0:T(4,128)} %convert_element_type.104, f32[9,36,4,128]{3,1,2,0:T(8,128)S(1)} %copy.49, f32[9,36,4,127]{3,1,2,0:T(8,128)} %get-tuple-element.22, f32[9,36]{1,0:T(8,128)} %get-tuple-element.52, ...), kind=kLoop, calls=%fused_computation.50 | loop fusion | flops 2819584 | bytes 3314116 | tf_op jit(solution)/shard_map/reduce_sum | solution.py:201
  58.6 0.9 fusion.57
  59.5 3.6 %collective-permute-start.2 = (f32[5,36,4,128]{3,1,2,0:T(8,128)}, f32[5,36,4,128]{3,1,2,0:T(8,128)S(1)}, u32[]{:S(2)}, u32[]{:S(2)}) collective-permute-start(f32[5,36,4,128]{3,1,2,0:T(8,128)} %get-tuple-element.17), channel_id=1, source_target_pairs={{0,1},{1,2},{2,3},{4,5},{5,6},{6,7},{8,9},{9,10},{10,11},{12,13},{... | collective-permute-start | bytes 1105928 | tf_op jit(solution)/shard_map/ppermute | solution.py:32
  63.2 1.9 %collective-permute-start.3 = (f32[5,36,4,128]{3,1,2,0:T(8,128)}, f32[5,36,4,128]{3,1,2,0:T(8,128)S(1)}, u32[]{:S(2)}, u32[]{:S(2)}) collective-permute-start(f32[5,36,4,128]{3,1,2,0:T(8,128)} %get-tuple-element.18), channel_id=1, source_target_pairs={{1,0},{2,1},{3,2},{5,4},{6,5},{7,6},{9,8},{10,9},{11,10},{13,12},{... | collective-permute-start | bytes 1105928 | tf_op jit(solution)/shard_map/ppermute | solution.py:33
  65.1 8.5 %psum.7 = f32[4,128]{1,0:T(4,128)S(1)} all-reduce(f32[4,128]{1,0:T(4,128)S(1)} %copy-done.11), channel_id=1, replica_groups=mesh['grid'=128,'spec'=4] {'spec'}, use_global_device_ids=true, to_apply=%region_1.0 | all-reduce | flops 512 | bytes 4096 | tf_op jit(solution)/shard_map/psum | solution.py:202
  73.6 0.9 broadcast_multiply_fusion.2
  74.5 0.9 broadcast_multiply_fusion.1
  76.7 0.9 subtract_multiply_fusion.1
  78.0 0.7 copy-done.3
  78.7 0.7 fusion.8
  79.4 2.2 %collective-permute-start.6 = (f32[9,36,1,128]{3,1,2,0:T(8,128)S(1)}, f32[9,36,1,128]{3,1,2,0:T(8,128)S(1)}, u32[]{:S(2)}, u32[]{:S(2)}) collective-permute-start(f32[9,36,1,128]{3,1,2,0:T(8,128)S(1)} %slice.266), channel_id=1, source_target_pairs={{4,0},{8,4},{12,8},{16,12},{20,16},{24,20},{28,24},{32,28},{36,32}... | collective-permute-start | bytes 497672 | tf_op jit(solution)/shard_map/ppermute | solution.py:41
  81.7 2.1 %fusion.28 = f32[9,36,4,128]{3,2,1,0:T(4,128)S(1)} fusion(f32[9,36,4,128]{3,2,1,0:T(4,128)S(1)} %copy-done, f32[9,36,1,128]{3,2,1,0:T(1,128)S(1)} %copy.57, f32[9,36,1,128]{3,2,1,0:T(1,128)S(1)} %copy.55, f32[9,36,4,127]{3,2,1,0:T(4,128)S(1)} %copy-done.1, f32[9,36,4,127]{3,2,1,0:T(4,128)S(1)} %get-tuple-element.23, f32[9,36]{1,0:T(8,128)S(1)} %copy-done.8, ...), kind=kLoop, calls=%fused_computation.60 | loop fusion | flops 2322432 | bytes 2980800 | tf_op jit(solution)/shard_map/sub | solution.py:85
  84.0 1.0 copy.63
  85.0 1.2 %collective-permute-done.6 = f32[9,36,1,128]{3,1,2,0:T(8,128)S(1)} collective-permute-done((f32[9,36,1,128]{3,1,2,0:T(8,128)S(1)}, f32[9,36,1,128]{3,1,2,0:T(8,128)S(1)}, u32[]{:S(2)}, u32[]{:S(2)}) %collective-permute-start.6) | collective-permute-done | bytes 165920 | tf_op jit(solution)/shard_map/ppermute | solution.py:41
  86.9 0.7 copy-done.2
  87.7 0.9 convolution_convert_fusion.1
  89.3 0.8 pad.8.send_ref
  90.1 19.2 %rim_exchange.1 = bf16[128,8,128]{2,1,0:T(8,128)(2,1)} custom-call(bf16[128,8,128]{2,1,0:T(8,128)(2,1)} %pad.8.send_ref), custom_call_target="tpu_custom_call" | custom-call | tf_op jit(solution)/shard_map/rim_exchange/pallas_call | solution.py:158
  109.3 1.1 reshape.522
  111.6 1.1 reshape.523
  (85 shorter events, 6.1 us)
Async XLA Ops:
  0.6 20.1 %copy-start = (f32[9,36,4,128]{3,2,1,0:T(4,128)S(1)}, f32[9,36,4,128]{3,2,1,0:T(4,128)}, u32[]{:S(2)}) copy-start(f32[9,36,4,128]{3,2,1,0:T(4,128)} %param.9) | copy-start | bytes 1990660
  1.9 53.4 %collective-permute-start = (f32[9,36,1,128]{3,1,2,0:T(8,128)S(1)}, f32[9,36,1,128]{3,1,2,0:T(8,128)S(1)}, u32[]{:S(2)}, u32[]{:S(2)}) collective-permute-start(f32[9,36,1,128]{3,1,2,0:T(8,128)S(1)} %get-tuple-element.19), channel_id=1, source_target_pairs={{0,4},{4,8},{8,12},{12,16},{16,20},{20,24},{24,28},{28,32},{32,36}... | collective-permute-start | bytes 497672 | tf_op jit(solution)/shard_map/ppermute | solution.py:32
  5.9 49.4 %collective-permute-start.1 = (f32[9,36,1,128]{3,1,2,0:T(8,128)S(1)}, f32[9,36,1,128]{3,1,2,0:T(8,128)S(1)}, u32[]{:S(2)}, u32[]{:S(2)}) collective-permute-start(f32[9,36,1,128]{3,1,2,0:T(8,128)S(1)} %get-tuple-element.20), channel_id=1, source_target_pairs={{4,0},{8,4},{12,8},{16,12},{20,16},{24,20},{28,24},{32,28},{36,32}... | collective-permute-start | bytes 497672 | tf_op jit(solution)/shard_map/ppermute | solution.py:33
  21.7 51.9 %collective-permute-start.4 = (f32[9,36,1,128]{3,1,2,0:T(8,128)}, f32[9,36,1,128]{3,1,2,0:T(8,128)}, u32[]{:S(2)}, u32[]{:S(2)}) collective-permute-start(f32[9,36,1,128]{3,1,2,0:T(8,128)} %copy.68), channel_id=1, source_target_pairs={{0,4},{4,8},{8,12},{12,16},{16,20},{20,24},{24,28},{28,32},{32,36}... | collective-permute-start | bytes 497672 | tf_op jit(solution)/shard_map/ppermute | solution.py:32
  24.2 50.2 %collective-permute-start.5 = (f32[9,36,1,128]{3,1,2,0:T(8,128)}, f32[9,36,1,128]{3,1,2,0:T(8,128)}, u32[]{:S(2)}, u32[]{:S(2)}) collective-permute-start(f32[9,36,1,128]{3,1,2,0:T(8,128)} %copy.69), channel_id=1, source_target_pairs={{4,0},{8,4},{12,8},{16,12},{20,16},{24,20},{28,24},{32,28},{36,32}... | collective-permute-start | bytes 497672 | tf_op jit(solution)/shard_map/ppermute | solution.py:33
  34.5 2.3 %copy-start.17 = (s32[128,1]{0,1:T(1,128)S(1)}, s32[128,1]{0,1:T(1,128)}, u32[]{:S(2)}) copy-start(s32[128,1]{0,1:T(1,128)} %param.13) | copy-start | bytes 1540
  55.3 0.7 copy-start.4
  55.3 0.7 copy-start.5
  58.6 6.5 %copy-start.11 = (f32[4,128]{1,0:T(4,128)S(1)}, f32[4,128]{1,0:T(4,128)}, u32[]{:S(2)}) copy-start(f32[4,128]{1,0:T(4,128)} %get-tuple-element.9) | copy-start | bytes 6148
  58.6 16.9 %copy-start.18 = (f32[9]{0:T(128)S(1)}, f32[9]{0:T(128)}, u32[]{:S(2)}) copy-start(f32[9]{0:T(128)} %get-tuple-element.56) | copy-start | bytes 112
  59.5 16.6 %collective-permute-start.2 = (f32[5,36,4,128]{3,1,2,0:T(8,128)}, f32[5,36,4,128]{3,1,2,0:T(8,128)S(1)}, u32[]{:S(2)}, u32[]{:S(2)}) collective-permute-start(f32[5,36,4,128]{3,1,2,0:T(8,128)} %get-tuple-element.17), channel_id=1, source_target_pairs={{0,1},{1,2},{2,3},{4,5},{5,6},{6,7},{8,9},{9,10},{10,11},{12,13},{... | collective-permute-start | bytes 1105928 | tf_op jit(solution)/shard_map/ppermute | solution.py:32
  63.2 12.8 %collective-permute-start.3 = (f32[5,36,4,128]{3,1,2,0:T(8,128)}, f32[5,36,4,128]{3,1,2,0:T(8,128)S(1)}, u32[]{:S(2)}, u32[]{:S(2)}) collective-permute-start(f32[5,36,4,128]{3,1,2,0:T(8,128)} %get-tuple-element.18), channel_id=1, source_target_pairs={{1,0},{2,1},{3,2},{5,4},{6,5},{7,6},{9,8},{10,9},{11,10},{13,12},{... | collective-permute-start | bytes 1105928 | tf_op jit(solution)/shard_map/ppermute | solution.py:33
  76.1 0.6 copy-start.20
  77.8 0.9 copy-start.3
  77.8 0.9 copy-start.19
  78.7 3.0 %copy-start.1 = (f32[9,36,4,127]{3,2,1,0:T(4,128)S(1)}, f32[9,36,4,127]{3,2,1,0:T(4,128)}, u32[]{:S(2)}) copy-start(f32[9,36,4,127]{3,2,1,0:T(4,128)} %get-tuple-element.24) | copy-start | bytes 1975108
  78.7 3.0 %copy-start.6 = (f32[9,36]{1,0:T(8,128)S(1)}, f32[9,36]{1,0:T(8,128)}, u32[]{:S(2)}) copy-start(f32[9,36]{1,0:T(8,128)} %get-tuple-element.43) | copy-start | bytes 3892
  78.7 3.0 %copy-start.7 = (f32[9,36]{1,0:T(8,128)S(1)}, f32[9,36]{1,0:T(8,128)}, u32[]{:S(2)}) copy-start(f32[9,36]{1,0:T(8,128)} %get-tuple-element.44) | copy-start | bytes 3892
  78.7 3.0 %copy-start.8 = (f32[9,36]{1,0:T(8,128)S(1)}, f32[9,36]{1,0:T(8,128)}, u32[]{:S(2)}) copy-start(f32[9,36]{1,0:T(8,128)} %get-tuple-element.54) | copy-start | bytes 3892
  78.7 3.0 %copy-start.9 = (f32[9,36]{1,0:T(8,128)S(1)}, f32[9,36]{1,0:T(8,128)}, u32[]{:S(2)}) copy-start(f32[9,36]{1,0:T(8,128)} %get-tuple-element.55) | copy-start | bytes 3892
  79.4 6.8 %collective-permute-start.6 = (f32[9,36,1,128]{3,1,2,0:T(8,128)S(1)}, f32[9,36,1,128]{3,1,2,0:T(8,128)S(1)}, u32[]{:S(2)}, u32[]{:S(2)}) collective-permute-start(f32[9,36,1,128]{3,1,2,0:T(8,128)S(1)} %slice.266), channel_id=1, source_target_pairs={{4,0},{8,4},{12,8},{16,12},{20,16},{24,20},{28,24},{32,28},{36,32}... | collective-permute-start | bytes 497672 | tf_op jit(solution)/shard_map/ppermute | solution.py:41
  86.7 1.0 copy-start.2
  86.9 1.7 %copy-start.12 = (bf16[128,1]{0,1:T(2,128)(2,1)S(1)}, bf16[128,1]{0,1:T(2,128)(2,1)}, u32[]{:S(2)}) copy-start(bf16[128,1]{0,1:T(2,128)(2,1)} %get-tuple-element.33) | copy-start | bytes 772
  86.9 1.7 %copy-start.13 = (bf16[128,1]{0,1:T(2,128)(2,1)S(1)}, bf16[128,1]{0,1:T(2,128)(2,1)}, u32[]{:S(2)}) copy-start(bf16[128,1]{0,1:T(2,128)(2,1)} %get-tuple-element.37) | copy-start | bytes 772
  86.9 1.7 %copy-start.15 = (bf16[128,1]{0,1:T(2,128)(2,1)S(1)}, bf16[128,1]{0,1:T(2,128)(2,1)}, u32[]{:S(2)}) copy-start(bf16[128,1]{0,1:T(2,128)(2,1)} %get-tuple-element.49) | copy-start | bytes 772
  86.9 1.7 %copy-start.16 = (bf16[128,1]{0,1:T(2,128)(2,1)S(1)}, bf16[128,1]{0,1:T(2,128)(2,1)}, u32[]{:S(2)}) copy-start(bf16[128,1]{0,1:T(2,128)(2,1)} %get-tuple-element.50) | copy-start | bytes 772
  86.9 1.8 %copy-start.14 = (pred[2,128]{1,0:T(4,128)(4,1)S(1)}, pred[2,128]{1,0:T(4,128)(4,1)}, u32[]{:S(2)}) copy-start(pred[2,128]{1,0:T(4,128)(4,1)} %iota_compare_fusion.6) | copy-start | bytes 772
  89.3 21.5 %copy-start.10 = (f32[512]{0:T(512)S(1)}, f32[512]{0:T(512)}, u32[]{:S(2)}) copy-start(f32[512]{0:T(512)} %iota_convert_fusion) | copy-start | bytes 6148

commit v2 on v0

v2 whole, which is shorter than its diff:
```python
import jax
import jax.numpy as jnp
import numpy as np
from jax import lax
from jax.experimental import pallas as pl
from jax.experimental.pallas import tpu as pltpu
from jax.sharding import PartitionSpec as P

FREQS = 36
ANGLES = 36
LON = 4
LAT = 128
RIM = 128
BANDS = 9
REACH = 5
BINS = BANDS * ANGLES
ROWS = BINS * LON
BAND_ROWS = ANGLES * LON
PAIRS = BAND_ROWS // 8
PACKET = 352
EAST = 336
WIDTH = 384
FACT = BINS - 256
MESH = pl.DeviceIdType.MESH
F32 = jnp.float32
BF16 = jnp.bfloat16

ratio_step = 1.1
speed_coef = 0.054
wind_coef = 0.05
dissip_coef = 0.2
nonlin_coef = 0.12
nest_speedup = 2.0


def tables():
    heading = 2.0 * np.pi * np.arange(ANGLES) / ANGLES
    cosine, sine = np.cos(heading), np.sin(heading)
    cosine[[9, 27]] = 0.0
    sine[[0, 18]] = 0.0

    def spread(x):
        rows = np.repeat(x, LON)
        return np.broadcast_to(rows[:, None], (BAND_ROWS, LAT)).astype(np.float32)

    degrees = -60.0 + 120.0 * (np.arange(LAT) + 0.5) / LAT
    secant = np.broadcast_to(1.0 / np.cos(degrees * np.pi / 180.0), (8, LAT)).astype(np.float32)
    bands = np.arange(-REACH, FREQS + REACH)
    ratio = ratio_step ** (bands - FREQS // 2).astype(np.float64)
    scalars = np.concatenate([ratio, 1.0 / ratio]).astype(np.float32)
    return spread(cosine), spread(sine), secant, scalars


RATIO_COUNT = FREQS + 2 * REACH
MEAN_SCALE = float(
    1.0 / (ANGLES * 0.1 * np.sum(ratio_step ** (np.arange(FREQS) - FREQS // 2.0)))
)


def dot_nt(a, b):
    return lax.dot_general(a, b, (((1,), (1,)), ((), ())), preferred_element_type=F32)


def split_16(x):
    high = x.astype(BF16)
    return high, (x - high.astype(F32)).astype(BF16)


def kernel(
    count,
    e_ref,
    n_ref,
    mask_ref,
    wind_ref,
    cell_ref,
    dest_ref,
    target_ref,
    weight_ref,
    cos_ref,
    sin_ref,
    sec_ref,
    scalar_ref,
    g_out,
    n_out,
    stage_a,
    stage_b,
    east_send,
    west_send,
    from_west,
    from_east,
    halo_e,
    halo_n,
    even,
    odd,
    bands_16,
    low_halo,
    high_halo,
    gain,
    nest,
    g_buf,
    n_buf,
    part,
    parts,
    col_send,
    col_recv,
    share_high,
    share_low,
    hot,
    facts,
    slot_rows,
    blocks,
    arrived,
    lon_send,
    lon_recv,
    band_send,
    band_recv,
    sum_send,
    sum_recv,
    col_ssem,
    col_rsem,
    rim_send,
    rim_recv,
    out_sem,
):
    me = lax.axis_index("grid")
    spec = lax.axis_index("spec")
    specs = FREQS // BANDS
    first = spec * BANDS
    west = lax.rem(me + count - 1, count)
    east = lax.rem(me + 1, count)
    barrier = pltpu.get_barrier_semaphore()

    def ratio(band):
        return scalar_ref[first + band]

    def inverse(band):
        return scalar_ref[first + band + RATIO_COUNT]

    def greet(i, carry):
        pl.semaphore_signal(
            barrier, inc=1, device_id={"grid": lax.rem(me + i, count)}, device_id_type=MESH
        )
        return carry

    lax.fori_loop(1, count, greet, 0)
    for i in range(1, specs):
        pl.semaphore_signal(
            barrier, inc=1, device_id={"spec": lax.rem(spec + i, specs)}, device_id_type=MESH
        )

    packet_rows = lax.broadcasted_iota(jnp.int32, (PACKET, LAT), 0)
    angle = lax.rem(packet_rows, ANGLES)
    eastward = (angle < 10) | (angle >= 28)
    stage_a[...] = jnp.zeros_like(stage_a)
    stage_b[...] = jnp.zeros_like(stage_b)
    for lon, picked, send in ((LON - 1, eastward, east_send), (0, ~eastward, west_send)):
        stage_a[pl.ds(0, BINS), :] = e_ref[pl.ds(lon, BINS, stride=LON), :]
        stage_b[pl.ds(18, BINS), :] = n_ref[pl.ds(lon, BINS, stride=LON), :]
        send[...] = jnp.where(picked, stage_a[...], stage_b[...]).astype(BF16)

    pl.semaphore_wait(barrier, count - 1 + specs - 1)

    def lon_copy(send, recv, index, to):
        return pltpu.make_async_remote_copy(
            src_ref=send,
            dst_ref=recv,
            send_sem=lon_send.at[index],
            recv_sem=lon_recv.at[index],
            device_id={"grid": to},
            device_id_type=MESH,
        )

    eastbound = lon_copy(east_send, from_west, 0, east)
    westbound = lon_copy(west_send, from_east, 1, west)
    eastbound.start()
    westbound.start()

    lane = lax.broadcasted_iota(jnp.int32, (RIM, LAT), 1)
    sub = lax.broadcasted_iota(jnp.int32, (RIM, LAT), 0)
    local_col = cell_ref[:, 0:1] - me * LON
    row = cell_ref[:, 1:2]
    ex = weight_ref[:, 0:1]
    ny = weight_ref[:, 1:2]
    relax = weight_ref[:, 2:3]
    row_share = jnp.where(lane == row, 1.0 - ny, jnp.where(lane == row + 1, ny, 0.0))
    for lon in range(LON + 1):
        col_share = jnp.where(
            local_col == lon, 1.0 - ex, jnp.where(local_col == lon - 1, ex, 0.0)
        )
        high, low = split_16(col_share * row_share)
        share_high[lon] = high
        share_low[lon] = low
    diagonal = lane == sub
    dest_col = dest_ref[...].astype(F32)
    dest_row = jnp.sum(jnp.where(diagonal, dest_col, 0.0), axis=0, keepdims=True)
    target_f = target_ref[...].astype(F32)
    target_col = jnp.sum(jnp.where(diagonal, target_f, 0.0), axis=1, keepdims=True).astype(jnp.int32)
    same = dest_col == dest_row
    slot_row = jnp.sum(jnp.where(same & (sub < lane), 1.0, 0.0), axis=0, keepdims=True)
    named = dest_row == sub.astype(F32)
    for j in range(2):
        hot[pl.ds(j * RIM, RIM), :] = jnp.where(named & (slot_row == float(j)), 1.0, 0.0).astype(BF16)
    relax_high = relax.astype(BF16).astype(F32)
    fact = jnp.where(lane == FACT, (target_col >> 7).astype(F32), 0.0)
    fact = jnp.where(lane == FACT + 1, (target_col & 127).astype(F32), fact)
    fact = jnp.where(lane == FACT + 2, relax_high, fact)
    fact = jnp.where(lane == FACT + 3, relax - relax_high, fact)
    facts[...] = fact
    slot_rows[...] = jnp.zeros_like(slot_rows)

    pair_shape = (PAIRS, 8, LAT)
    cosine = cos_ref[...].reshape(pair_shape)
    sine = sin_ref[...].reshape(pair_shape)
    wind = wind_ref[...]
    wind_x = jnp.concatenate([wind[0], wind[0]], axis=0)[None]
    wind_y = jnp.concatenate([wind[1], wind[1]], axis=0)[None]
    gain[...] = wind_coef * jnp.maximum(wind_x * cosine + wind_y * sine, 0.0)
    mask_half = mask_ref[...].astype(F32)
    mask = jnp.concatenate([mask_half, mask_half], axis=0)[None]
    secant = sec_ref[...][None]

    vreg_sub = lax.broadcasted_iota(jnp.int32, (1, 8, LAT), 1)
    vreg_lane = lax.broadcasted_iota(jnp.int32, (1, 8, LAT), 2)
    lon_of = vreg_sub & 3

    def upwind(block, halo):
        before = jnp.where(lon_of == 0, halo, pltpu.roll(block, 1, axis=1))
        after = jnp.where(lon_of == LON - 1, halo, pltpu.roll(block, 7, axis=1))
        along_lon = jnp.concatenate([before[:5], after[5:14], before[14:]], axis=0)
        south = jnp.where(vreg_lane == 0, 0.0, pltpu.roll(block, 1, axis=2))
        north = jnp.where(vreg_lane == LAT - 1, 0.0, pltpu.roll(block, LAT - 1, axis=2))
        along_lat = jnp.concatenate([south[:9], north[9:]], axis=0)
        return block - along_lon, block - along_lat

    def rows_of(ref, band):
        return ref[pl.ds(pl.multiple_of(band * BAND_ROWS, 8), BAND_ROWS), :].reshape(pair_shape)

    def cyclic(ref, band, value):
        ref[band, pl.ds(2, PAIRS)] = value
        ref[band, pl.ds(0, 2)] = value[PAIRS - 2 :]
        ref[band, pl.ds(PAIRS + 2, 2)] = value[:2]

    def keep(band, value):
        cyclic(even, band, value)
        turned = pltpu.roll(value, 4, axis=1)
        following = jnp.concatenate([turned[1:], turned[:1]], axis=0)
        cyclic(odd, band, jnp.where(vreg_sub < 4, turned, following))

    eastbound.wait()
    westbound.wait()
    stage_a[...] = from_west[...].astype(F32)
    stage_b[...] = from_east[...].astype(F32)
    quarter = count // 4
    lower_keep = jnp.where((me != quarter) & (me != 3 * quarter), 1.0, 0.0)
    upper_keep = jnp.where((me != quarter - 1) & (me != 3 * quarter - 1), 1.0, 0.0)
    halo_e[pl.ds(0, BINS, stride=LON), :] = stage_a[pl.ds(0, BINS), :]
    halo_e[pl.ds(LON - 1, BINS, stride=LON), :] = stage_b[pl.ds(0, BINS), :]
    halo_n[pl.ds(0, BINS, stride=LON), :] = stage_a[pl.ds(18, BINS), :] * lower_keep
    halo_n[pl.ds(LON - 1, BINS, stride=LON), :] = stage_b[pl.ds(18, BINS), :] * upper_keep

    def advect_band(band, total):
        block = rows_of(e_ref, band)
        lon_step, lat_step = upwind(block, rows_of(halo_e, band))
        speed = speed_coef * inverse(band + REACH)
        along_x = jnp.abs(rows_of(cos_ref, 0)) * secant
        along_y = jnp.abs(rows_of(sin_ref, 0))
        moved = (block - speed * (along_x * lon_step + along_y * lat_step)) * mask
        keep(band + REACH, moved)
        bands_16[band] = moved.reshape(BAND_ROWS, LAT).astype(BF16)
        return total + 0.1 * ratio(band + REACH) * jnp.sum(moved, axis=0)

    part[...] = lax.fori_loop(0, BANDS, advect_band, jnp.zeros((8, LAT), F32))

    def band_copy(start, recv, index, to):
        return pltpu.make_async_remote_copy(
            src_ref=bands_16.at[pl.ds(start, REACH)],
            dst_ref=recv,
            send_sem=band_send.at[index],
            recv_sem=band_recv.at[index],
            device_id={"spec": to},
            device_id_type=MESH,
        )

    upward = band_copy(BANDS - REACH, low_halo, 0, lax.rem(spec + 1, specs))
    downward = band_copy(0, high_halo, 1, lax.rem(spec + specs - 1, specs))

    @pl.when(spec < specs - 1)
    def _():
        upward.start()

    @pl.when(spec > 0)
    def _():
        downward.start()

    sums = []
    for i in range(1, specs):
        sums.append(
            pltpu.make_async_remote_copy(
                src_ref=part,
                dst_ref=parts.at[i],
                send_sem=sum_send.at[i],
                recv_sem=sum_recv.at[i],
                device_id={"spec": lax.rem(spec + i, specs)},
                device_id_type=MESH,
            )
        )
    for copy in sums:
        copy.start()

    def advect_nest(band, carry):
        block = rows_of(n_ref, band)
        lon_step, lat_step = upwind(block, rows_of(halo_n, band))
        speed = nest_speedup * speed_coef * inverse(band + REACH)
        along_x = jnp.abs(rows_of(cos_ref, 0))
        along_y = jnp.abs(rows_of(sin_ref, 0))
        moved = block - speed * (along_x * lon_step + along_y * lat_step)
        nest[pl.ds(pl.multiple_of(band * BAND_ROWS, 8), BAND_ROWS), :] = moved.reshape(BAND_ROWS, LAT)
        return carry

    lax.fori_loop(0, BANDS, advect_nest, 0)

    @pl.when(spec < specs - 1)
    def _():
        upward.wait_send()
        downward.wait_recv()

    @pl.when(spec > 0)
    def _():
        upward.wait_recv()
        downward.wait_send()

    def halo_bands(band, carry):
        low = low_halo[band].astype(F32).reshape(pair_shape)
        keep(band, jnp.where(spec > 0, low, 0.0))
        high = high_halo[band].astype(F32).reshape(pair_shape)
        keep(band + BANDS + REACH, jnp.where(spec < specs - 1, high, 0.0))
        return carry

    lax.fori_loop(0, REACH, halo_bands, 0)

    chunk = 6

    def nonlinear_band(band, carry):
        for piece in range(PAIRS // chunk):
            base = 2 + piece * chunk

            def at(ref, offset, turn):
                return ref[band + REACH + offset, pl.ds(base + turn, chunk)]

            here = at(even, 0, 0)
            total = here * (1.0 + ratio(band + REACH) * gain[pl.ds(piece * chunk, chunk)])

            def product(centre, upper, lower):
                return centre * (centre * (upper + lower) - 2.0 * upper * lower)

            own = 0.0
            below = 0.0
            above = 0.0
            for s in (1, -1):
                own += product(
                    here, at(odd, 2, (3 * s - 1) // 2), at(odd, -3, (-s - 1) // 2)
                )
                below += product(at(odd, -2, (-3 * s - 1) // 2), here, at(even, -5, -2 * s))
                above += product(at(odd, 3, (s - 1) // 2), at(even, 5, 2 * s), here)
            total += nonlin_coef * (
                ratio(band + REACH - 2) * below
                + ratio(band + REACH + 3) * above
                - 2.0 * ratio(band + REACH) * own
            )
            start = pl.multiple_of(band * BAND_ROWS + piece * chunk * 8, 8)
            g_buf[pl.ds(start, chunk * 8), :] = total.reshape(chunk * 8, LAT)
        return carry

    lax.fori_loop(0, BANDS, nonlinear_band, 0)

    for copy in sums:
        copy.wait()
    whole = part[...] + parts[1] + parts[2] + parts[3]
    mean = (whole + pltpu.roll(whole, 4, axis=0)) * MEAN_SCALE

    def damp_band(band, carry):
        value = ratio(band + REACH)
        inverse_loss = 1.0 / (1.0 + dissip_coef * value * value * mean)
        start = pl.multiple_of(band * BAND_ROWS, 8)
        result = rows_of(g_buf, band) * inverse_loss[None]
        g_buf[pl.ds(start, BAND_ROWS), :] = result.reshape(BAND_ROWS, LAT)
        return carry

    lax.fori_loop(0, BANDS, damp_band, 0)
    g_buf[pl.ds(ROWS, WIDTH * LON - ROWS), :] = jnp.zeros((WIDTH * LON - ROWS, LAT), F32)

    col_send[...] = g_buf[pl.ds(0, WIDTH, stride=LON), :].astype(BF16)
    column = pltpu.make_async_remote_copy(
        src_ref=col_send,
        dst_ref=col_recv,
        send_sem=col_ssem,
        recv_sem=col_rsem,
        device_id={"grid": west},
        device_id_type=MESH,
    )
    column.start()
    g_copy = pltpu.make_async_copy(g_buf.at[pl.ds(0, ROWS)], g_out, out_sem.at[0])
    g_copy.start()

    boundary = jnp.zeros((RIM, WIDTH), F32)
    for lon in range(LON):
        high, low = split_16(g_buf[pl.ds(lon, WIDTH, stride=LON), :])
        boundary += dot_nt(share_high[lon], high)
        boundary += dot_nt(share_high[lon], low)
        boundary += dot_nt(share_low[lon], high)
    column.wait()
    boundary += dot_nt(share_high[LON], col_recv[...])
    boundary += dot_nt(share_low[LON], col_recv[...])
    boundary = jnp.concatenate([boundary[:, :256], boundary[:, 256:] + facts[...]], axis=1)
    packed = jnp.dot(hot[...], boundary.astype(BF16), preferred_element_type=F32)
    for j in range(2):
        for c in range(3):
            slot_rows[pl.ds(j * 3 + c, RIM, stride=8), :] = packed[
                j * RIM : (j + 1) * RIM, c * LAT : (c + 1) * LAT
            ]
    blocks[...] = slot_rows[...].reshape(count, 8, LAT).astype(BF16)

    own_block = pltpu.make_async_copy(blocks.at[me], arrived.at[me], rim_recv)
    own_block.start()

    def post(i, carry):
        dest = lax.rem(me + i, count)
        pltpu.make_async_remote_copy(
            src_ref=blocks.at[dest],
            dst_ref=arrived.at[me],
            send_sem=rim_send,
            recv_sem=rim_recv,
            device_id={"grid": dest},
            device_id_type=MESH,
        ).start()
        return carry

    lax.fori_loop(1, count, post, 0)
    others = blocks.at[pl.ds(0, count - 1)]
    pltpu.make_async_copy(others, others, rim_send).wait()
    pltpu.make_async_copy(arrived, arrived, rim_recv).wait()

    slot_rows[...] = arrived[...].astype(F32).reshape(count * 8, LAT)
    halves = []
    for j in range(2):
        halves.append(
            jnp.concatenate(
                [slot_rows[pl.ds(j * 3 + c, RIM, stride=8), :] for c in range(3)], axis=1
            )
        )
    spectra = jnp.concatenate(halves, axis=0)
    told = spectra[:, 256:]
    cell = told[:, FACT : FACT + 1] * float(LAT) + told[:, FACT + 1 : FACT + 2]
    cells = lax.broadcasted_iota(jnp.int32, (2 * RIM, LON * LAT), 1).astype(F32)
    hit = cell == cells
    rate_high = jnp.where(hit, told[:, FACT + 2 : FACT + 3], 0.0)
    rate_low = jnp.where(hit, told[:, FACT + 3 : FACT + 4], 0.0)
    remains = 1.0 - jnp.sum(rate_high + rate_low, axis=0, keepdims=True)
    turned = spectra.T.astype(BF16)
    gained = jnp.dot(turned, rate_high.astype(BF16), preferred_element_type=F32)
    gained += jnp.dot(turned, rate_low.astype(BF16), preferred_element_type=F32)
    for lon in range(LON):
        lanes = slice(lon * LAT, (lon + 1) * LAT)
        held = nest[pl.ds(lon, BINS, stride=LON), :]
        n_buf[pl.ds(lon, BINS, stride=LON), :] = held * remains[:, lanes] + gained[:BINS, lanes]
    n_copy = pltpu.make_async_copy(n_buf, n_out, out_sem.at[1])
    n_copy.start()
    g_copy.wait()
    n_copy.wait()


def per_device(
    energy, nest_energy, ocean_mask, wind_field, rim_cell, rim_dest, rim_target, rim_weight
):
    count = lax.axis_size("grid")
    cosine, sine, secant, scalars = tables()
    vmem = pl.BlockSpec(memory_space=pltpu.VMEM)
    flat = jax.ShapeDtypeStruct((ROWS, LAT), F32)
    dma = pltpu.SemaphoreType.DMA

    def body(*refs):
        kernel(count, *refs)

    global_next, nest_next = pl.pallas_call(
        body,
        out_shape=(flat, flat),
        in_specs=[vmem] * 11 + [pl.BlockSpec(memory_space=pltpu.SMEM)],
        out_specs=(pl.BlockSpec(memory_space=pl.ANY), pl.BlockSpec(memory_space=pl.ANY)),
        scratch_shapes=[
            pltpu.VMEM((PACKET, LAT), F32),
            pltpu.VMEM((PACKET, LAT), F32),
            pltpu.VMEM((PACKET, LAT), BF16),
            pltpu.VMEM((PACKET, LAT), BF16),
            pltpu.VMEM((PACKET, LAT), BF16),
            pltpu.VMEM((PACKET, LAT), BF16),
            pltpu.VMEM((ROWS, LAT), F32),
            pltpu.VMEM((ROWS, LAT), F32),
            pltpu.VMEM((BANDS + 2 * REACH, PAIRS + 4, 8, LAT), F32),
            pltpu.VMEM((BANDS + 2 * REACH, PAIRS + 4, 8, LAT), F32),
            pltpu.VMEM((BANDS, BAND_ROWS, LAT), BF16),
            pltpu.VMEM((REACH, BAND_ROWS, LAT), BF16),
            pltpu.VMEM((REACH, BAND_ROWS, LAT), BF16),
            pltpu.VMEM((PAIRS, 8, LAT), F32),
            pltpu.VMEM((ROWS, LAT), F32),
            pltpu.VMEM((WIDTH * LON, LAT), F32),
            pltpu.VMEM((ROWS, LAT), F32),
            pltpu.VMEM((8, LAT), F32),
            pltpu.VMEM((4, 8, LAT), F32),
            pltpu.VMEM((WIDTH, LAT), BF16),
            pltpu.VMEM((WIDTH, LAT), BF16),
            pltpu.VMEM((LON + 1, RIM, LAT), BF16),
            pltpu.VMEM((LON + 1, RIM, LAT), BF16),
            pltpu.VMEM((2 * RIM, RIM), BF16),
            pltpu.VMEM((RIM, LAT), F32),
            pltpu.VMEM((count * 8, LAT), F32),
            pltpu.VMEM((count, 8, LAT), BF16),
            pltpu.VMEM((count, 8, LAT), BF16),
            dma((2,)),
            dma((2,)),
            dma((2,)),
            dma((2,)),
            dma((4,)),
            dma((4,)),
            dma,
            dma,
            dma,
            dma,
            dma((2,)),
        ],
        compiler_params=pltpu.CompilerParams(
            collective_id=0, has_side_effects=True, vmem_limit_bytes=40 << 20
        ),
        name="wave_step",
    )(
        energy.reshape(ROWS, LAT),
        nest_energy.reshape(ROWS, LAT),
        ocean_mask,
        wind_field,
        rim_cell,
        rim_dest,
        rim_target.reshape(1, RIM),
        rim_weight,
        jnp.asarray(cosine),
        jnp.asarray(sine),
        jnp.asarray(secant),
        jnp.asarray(scalars),
    )
    shape = energy.shape
    return (global_next.reshape(shape), nest_next.reshape(shape))


def solution(mesh):
    in_specs = (
        P("spec", None, "grid", None),
        P("spec", None, "grid", None),
        P("grid", None),
        P(None, "grid", None),
        P("grid", None),
        P("grid", None),
        P("grid"),
        P("grid", None),
    )
    out_specs = (P("spec", None, "grid", None), P("spec", None, "grid", None))
    return jax.shard_map(
        per_device, mesh=mesh, in_specs=in_specs, out_specs=out_specs, check_vma=False
    )
```

time: 1310 us -> 56.3 us (0.04)
  the two profiles are of different devices: /device:TPU:2 before, /device:TPU:1 now
where the time goes in v2:
time: 56.3 us; the launch traced here: 55.7 us
  Pallas kernels  49.1 us (87%)
  local copies, waits for them, and re-layouts  5.91 us (10%)
  between operations  0.69 us (1%)
    pallas_call x1, Pallas kernels, per_device(): pl.pallas_call(body, out_shape=(flat, flat), in_specs=[vmem] * 11 + [pl.B...  49.1 us
    unnamed x29, local copies, waits for them, and re-layouts  5.91 us

profile of v2, /device:TPU:1, one launch (start us, length us, event | category | flops | bytes accessed | tf_op | source)
XLA Modules:
  0.0 55.7 jit_solution(9031560631199571101)
XLA Ops:
  0.6 0.0 copy-start.10
  0.6 0.0 copy-start.11
  0.7 0.7 %copy-done.10 = s32[128,2]{0,1:T(2,128)S(1)} copy-done((s32[128,2]{0,1:T(2,128)S(1)}, s32[128,2]{0,1:T(2,128)}, u32[]{:S(2)}) %copy-start.10) | copy-done | bytes 1048
  1.3 0.0 copy-start.9
  1.3 0.0 copy-start.3
  1.3 0.1 copy.14.refs_4_
  1.4 0.0 copy-done.11
  1.4 0.0 copy-start.2
  1.4 0.1 copy.15.refs_5_
  1.6 0.4 copy-done.9
  2.0 0.0 copy-start.4
  2.0 0.0 copy-start.5
  2.0 0.0 copy-start.6
  2.0 0.0 copy-start.7
  2.0 0.0 copy-start.8
  2.0 0.1 copy.16.refs_7_
  2.1 0.1 copy-done.3
  2.2 0.1 copy-done.2
  2.3 0.4 copy-done.4
  2.7 0.0 copy-done.5
  2.7 0.0 copy-done.6
  2.7 0.0 copy-done.7
  2.7 0.0 copy-done.8
  2.7 0.0 copy-start
  2.7 1.1 %copy-done = f32[9,36,4,128]{3,2,1,0:T(4,128)S(1)} copy-done((f32[9,36,4,128]{3,2,1,0:T(4,128)S(1)}, f32[9,36,4,128]{3,2,1,0:T(4,128)}, u32[]{:S(2)}) %copy-start) | copy-done | bytes 663576
  3.8 0.0 copy-start.1
  3.8 1.1 %copy-done.1 = f32[9,36,4,128]{3,2,1,0:T(4,128)S(1)} copy-done((f32[9,36,4,128]{3,2,1,0:T(4,128)S(1)}, f32[9,36,4,128]{3,2,1,0:T(4,128)}, u32[]{:S(2)}) %copy-start.1) | copy-done | bytes 663576
  4.9 49.1 %wave_step.1 = (f32[1296,128]{1,0:T(8,128)S(1)}, f32[1296,128]{1,0:T(8,128)S(1)}) custom-call(f32[1296,128]{1,0:T(8,128)S(1)} %bitcast.7, f32[1296,128]{1,0:T(8,128)S(1)} %bitcast.8, s32[4,128]{1,0:T(4,128)S(1)} %copy-done.6, f32[2,4,128]{2,1,0:T(4,128)S(1)} %copy-done.4, s32[128,2]{1,0:T(8,128)S(1)} %copy.14.refs_4_, s32[128,1]{1,0:T(8,128)S(1)} %copy.15.refs_5_, ...), custom_call_target="tpu_custom_call" | custom-call | tf_op jit(solution)/shard_map/wave_step/pallas_call | solution.py:484
  54.1 0.8 %copy.19 = f32[9,36,4,128]{3,2,1,0:T(4,128)} copy(f32[9,36,4,128]{3,2,1,0:T(4,128)S(1)} %bitcast.6) | data formatting | bytes 1327104
  54.9 0.8 %copy.20 = f32[9,36,4,128]{3,2,1,0:T(4,128)} copy(f32[9,36,4,128]{3,2,1,0:T(4,128)S(1)} %bitcast.5) | data formatting | bytes 1327104
Async XLA Ops:
  0.6 0.7 %copy-start.10 = (s32[128,2]{0,1:T(2,128)S(1)}, s32[128,2]{0,1:T(2,128)}, u32[]{:S(2)}) copy-start(s32[128,2]{0,1:T(2,128)} %param.16) | copy-start | bytes 3076
  0.6 0.8 %copy-start.11 = (s32[128,1]{0,1:T(1,128)S(1)}, s32[128,1]{0,1:T(1,128)}, u32[]{:S(2)}) copy-start(s32[128,1]{0,1:T(1,128)} %param.17) | copy-start | bytes 1540
  1.3 0.7 %copy-start.9 = (f32[128,3]{0,1:T(4,128)S(1)}, f32[128,3]{0,1:T(4,128)}, u32[]{:S(2)}) copy-start(f32[128,3]{0,1:T(4,128)} %param.19) | copy-start | bytes 4612
  1.3 0.9 %copy-start.3 = (f32[144,128]{1,0:T(8,128)S(1)}, f32[144,128]{1,0:T(8,128)}, u32[]{:S(2)}) copy-start(f32[144,128]{1,0:T(8,128)} %constant.8.clone.refs_8_) | copy-start | bytes 221188
  1.4 0.9 %copy-start.2 = (f32[144,128]{1,0:T(8,128)S(1)}, f32[144,128]{1,0:T(8,128)}, u32[]{:S(2)}) copy-start(f32[144,128]{1,0:T(8,128)} %constant.9.clone.refs_9_) | copy-start | bytes 221188
  2.0 0.7 %copy-start.4 = (f32[2,4,128]{2,1,0:T(4,128)S(1)}, f32[2,4,128]{2,1,0:T(4,128)}, u32[]{:S(2)}) copy-start(f32[2,4,128]{2,1,0:T(4,128)} %refs_3_.1) | copy-start | bytes 12292
  2.0 0.7 %copy-start.5 = (f32[8,128]{1,0:T(8,128)S(1)}, f32[8,128]{1,0:T(8,128)}, u32[]{:S(2)}) copy-start(f32[8,128]{1,0:T(8,128)} %constant.10.clone.refs_10_) | copy-start | bytes 12292
  2.0 0.7 %copy-start.6 = (s32[4,128]{1,0:T(4,128)S(1)}, s32[4,128]{1,0:T(4,128)}, u32[]{:S(2)}) copy-start(s32[4,128]{1,0:T(4,128)} %refs_2_.1) | copy-start | bytes 6148
  2.0 0.7 %copy-start.7 = (s32[128]{0:T(128)S(1)}, s32[128]{0:T(128)}, u32[]{:S(2)}) copy-start(s32[128]{0:T(128)} %param.18) | copy-start | bytes 1540
  2.0 0.7 %copy-start.8 = (f32[92]{0:T(128)S(1)}, f32[92]{0:T(128)}, u32[]{:S(2)}) copy-start(f32[92]{0:T(128)} %constant.11.clone.refs_11_) | copy-start | bytes 1108
  2.7 1.1 %copy-start = (f32[9,36,4,128]{3,2,1,0:T(4,128)S(1)}, f32[9,36,4,128]{3,2,1,0:T(4,128)}, u32[]{:S(2)}) copy-start(f32[9,36,4,128]{3,2,1,0:T(4,128)} %param.12) | copy-start | bytes 1990660
  3.8 1.1 %copy-start.1 = (f32[9,36,4,128]{3,2,1,0:T(4,128)S(1)}, f32[9,36,4,128]{3,2,1,0:T(4,128)}, u32[]{:S(2)}) copy-start(f32[9,36,4,128]{3,2,1,0:T(4,128)} %param.13) | copy-start | bytes 1990660

commit v3 on v2

--- a/solution.py
+++ b/solution.py
@@ -17,8 +17,10 @@
 ROWS = BINS * LON
 BAND_ROWS = ANGLES * LON
 PAIRS = BAND_ROWS // 8
-PACKET = 352
+PACKET = 208
+FIRST_ROWS = 144
 EAST = 336
+RING = 8
 WIDTH = 384
 FACT = BINS - 256
 MESH = pl.DeviceIdType.MESH
@@ -47,7 +49,8 @@
     secant = np.broadcast_to(1.0 / np.cos(degrees * np.pi / 180.0), (8, LAT)).astype(np.float32)
     bands = np.arange(-REACH, FREQS + REACH)
     ratio = ratio_step ** (bands - FREQS // 2).astype(np.float64)
-    scalars = np.concatenate([ratio, 1.0 / ratio]).astype(np.float32)
+    scalars = np.zeros((128,), np.float32)
+    scalars[: 2 * ratio.size] = np.concatenate([ratio, 1.0 / ratio])
     return spread(cosine), spread(sine), secant, scalars
 
 
@@ -66,8 +69,31 @@
     return high, (x - high.astype(F32)).astype(BF16)
 
 
+def far_first():
+    def hops(step):
+        z, x, y = step
+        return min(z, RING - z) + 2 * x + min(y, RING - y)
+
+    steps = [(z, x, y) for z in range(RING) for x in range(2) for y in range(RING)]
+    return sorted(steps[1:], key=lambda step: -hops(step))
+
+
 def kernel(
     count,
+    e_hbm,
+    n_hbm,
+    mask_hbm,
+    wind_hbm,
+    cell_hbm,
+    dest_hbm,
+    target_hbm,
+    weight_hbm,
+    cos_hbm,
+    sin_hbm,
+    sec_hbm,
+    scalar_hbm,
+    g_out,
+    n_out,
     e_ref,
     n_ref,
     mask_ref,
@@ -80,14 +106,13 @@
     sin_ref,
     sec_ref,
     scalar_ref,
-    g_out,
-    n_out,
+    rim_rows,
     stage_a,
     stage_b,
-    east_send,
-    west_send,
-    from_west,
-    from_east,
+    e_send,
+    n_send,
+    e_recv,
+    n_recv,
     halo_e,
     halo_n,
     even,
@@ -98,7 +123,6 @@
     gain,
     nest,
     g_buf,
-    n_buf,
     part,
     parts,
     col_send,
@@ -110,6 +134,7 @@
     slot_rows,
     blocks,
     arrived,
+    in_sem,
     lon_send,
     lon_recv,
     band_send,
@@ -120,8 +145,23 @@
     col_rsem,
     rim_send,
     rim_recv,
-    out_sem,
+    ring_sem,
+    half_sem,
 ):
+    sources = (
+        e_hbm, n_hbm, scalar_hbm, mask_hbm, cos_hbm, sin_hbm, sec_hbm, wind_hbm,
+        cell_hbm, dest_hbm, target_hbm, weight_hbm,
+    )
+    places = (
+        e_ref, n_ref, scalar_ref, mask_ref, cos_ref, sin_ref, sec_ref, wind_ref,
+        cell_ref, dest_ref, target_ref, weight_ref,
+    )
+    loads = [
+        pltpu.make_async_copy(source, place, in_sem.at[i])
+        for i, (source, place) in enumerate(zip(sources, places))
+    ]
+    loads[0].start()
+    loads[1].start()
     me = lax.axis_index("grid")
     spec = lax.axis_index("spec")
     specs = FREQS // BANDS
@@ -136,52 +176,92 @@
     def inverse(band):
         return scalar_ref[first + band + RATIO_COUNT]
 
-    def greet(i, carry):
-        pl.semaphore_signal(
-            barrier, inc=1, device_id={"grid": lax.rem(me + i, count)}, device_id_type=MESH
-        )
-        return carry
-
-    lax.fori_loop(1, count, greet, 0)
+    z_part = me // (2 * RING)
+    x_part = lax.rem(me // RING, 2)
+    y_part = lax.rem(me, RING)
+
+    def place_of(z, x, y):
+        return (z * 2 + x) * RING + y
+
+    def turned_by(part, step, size):
+        return lax.rem(part + step, size) if step else part
+
+    def tell(sem, to):
+        pl.semaphore_signal(sem, inc=1, device_id=to, device_id_type=MESH)
+
+    tell(barrier, {"grid": west})
+    tell(barrier, {"grid": east})
     for i in range(1, specs):
-        pl.semaphore_signal(
-            barrier, inc=1, device_id={"spec": lax.rem(spec + i, specs)}, device_id_type=MESH
-        )
+        tell(barrier, {"spec": lax.rem(spec + i, specs)})
+    z_peers = [place_of(turned_by(z_part, i, RING), x_part, y_part) for i in range(1, RING)]
+    x_peer = place_of(z_part, 1 - x_part, y_part)
+    for i in range(1, RING):
+        tell(barrier, {"grid": place_of(z_part, x_part, turned_by(y_part, i, RING))})
+    for peer in z_peers:
+        tell(barrier, {"grid": peer})
+    tell(barrier, {"grid": x_peer})
+    for load in loads[2:]:
+        load.start()
 
     packet_rows = lax.broadcasted_iota(jnp.int32, (PACKET, LAT), 0)
     angle = lax.rem(packet_rows, ANGLES)
     eastward = (angle < 10) | (angle >= 28)
     stage_a[...] = jnp.zeros_like(stage_a)
     stage_b[...] = jnp.zeros_like(stage_b)
-    for lon, picked, send in ((LON - 1, eastward, east_send), (0, ~eastward, west_send)):
-        stage_a[pl.ds(0, BINS), :] = e_ref[pl.ds(lon, BINS, stride=LON), :]
-        stage_b[pl.ds(18, BINS), :] = n_ref[pl.ds(lon, BINS, stride=LON), :]
-        send[...] = jnp.where(picked, stage_a[...], stage_b[...]).astype(BF16)
-
-    pl.semaphore_wait(barrier, count - 1 + specs - 1)
-
-    def lon_copy(send, recv, index, to):
-        return pltpu.make_async_remote_copy(
-            src_ref=send,
-            dst_ref=recv,
-            send_sem=lon_send.at[index],
-            recv_sem=lon_recv.at[index],
-            device_id={"grid": to},
-            device_id_type=MESH,
-        )
-
-    eastbound = lon_copy(east_send, from_west, 0, east)
-    westbound = lon_copy(west_send, from_east, 1, west)
-    eastbound.start()
-    westbound.start()
+    direct = 5 * ANGLES
+    folded = BINS - direct
+
+    def pack(source, send):
+        for index, lon, picked in ((0, LON - 1, eastward), (1, 0, ~eastward)):
+            stage_a[pl.ds(0, direct), :] = source[pl.ds(lon, direct, stride=LON), :]
+            stage_b[pl.ds(18, folded), :] = source[pl.ds(direct * LON + lon, folded, stride=LON), :]
+            send[index] = jnp.where(picked, stage_a[...], stage_b[...]).astype(BF16)
+
+    loads[0].wait()
+    pack(e_ref, e_send)
+    pl.semaphore_wait(barrier, 2 + specs - 1 + 2 * (RING - 1) + 1)
+
+    def lon_copies(send, recv, base):
+        return [
+            pltpu.make_async_remote_copy(
+                src_ref=send.at[index],
+                dst_ref=recv.at[index],
+                send_sem=lon_send.at[base + index],
+                recv_sem=lon_recv.at[base + index],
+                device_id={"grid": to},
+                device_id_type=MESH,
+            )
+            for index, to in ((0, east), (1, west))
+        ]
+
+    e_lon = lon_copies(e_send, e_recv, 0)
+    n_lon = lon_copies(n_send, n_recv, 2)
+    for copy in e_lon:
+        copy.start()
+    for peer in z_peers:
+        tell(ring_sem, {"grid": peer})
+    loads[1].wait()
+    pack(n_ref, n_send)
+    for copy in n_lon:
+        copy.start()
+    for load in loads[2:]:
+        load.wait()
 
     lane = lax.broadcasted_iota(jnp.int32, (RIM, LAT), 1)
     sub = lax.broadcasted_iota(jnp.int32, (RIM, LAT), 0)
-    local_col = cell_ref[:, 0:1] - me * LON
-    row = cell_ref[:, 1:2]
-    ex = weight_ref[:, 0:1]
-    ny = weight_ref[:, 1:2]
-    relax = weight_ref[:, 2:3]
+    rim_rows[...] = jnp.zeros_like(rim_rows)
+    rim_rows[pl.ds(0, 2), :] = cell_ref[...].astype(F32)
+    rim_rows[pl.ds(2, 1), :] = dest_ref[...].astype(F32)
+    rim_rows[pl.ds(3, 1), :] = target_ref[...].astype(F32)
+    rim_rows[pl.ds(4, 3), :] = weight_ref[...]
+    rim_cols = rim_rows[...].T
+    local_col = rim_cols[:, 0:1].astype(jnp.int32) - me * LON
+    row = rim_cols[:, 1:2].astype(jnp.int32)
+    dest_col = rim_cols[:, 2:3]
+    target_col = rim_cols[:, 3:4].astype(jnp.int32)
+    ex = rim_cols[:, 4:5]
+    ny = rim_cols[:, 5:6]
+    relax = rim_cols[:, 6:7]
     row_share = jnp.where(lane == row, 1.0 - ny, jnp.where(lane == row + 1, ny, 0.0))
     for lon in range(LON + 1):
         col_share = jnp.where(
@@ -190,11 +270,7 @@
         high, low = split_16(col_share * row_share)
         share_high[lon] = high
         share_low[lon] = low
-    diagonal = lane == sub
-    dest_col = dest_ref[...].astype(F32)
-    dest_row = jnp.sum(jnp.where(diagonal, dest_col, 0.0), axis=0, keepdims=True)
-    target_f = target_ref[...].astype(F32)
-    target_col = jnp.sum(jnp.where(diagonal, target_f, 0.0), axis=1, keepdims=True).astype(jnp.int32)
+    dest_row = dest_ref[...].astype(F32)
     same = dest_col == dest_row
     slot_row = jnp.sum(jnp.where(same & (sub < lane), 1.0, 0.0), axis=0, keepdims=True)
     named = dest_row == sub.astype(F32)
@@ -246,17 +322,19 @@
         following = jnp.concatenate([turned[1:], turned[:1]], axis=0)
         cyclic(odd, band, jnp.where(vreg_sub < 4, turned, following))
 
-    eastbound.wait()
-    westbound.wait()
-    stage_a[...] = from_west[...].astype(F32)
-    stage_b[...] = from_east[...].astype(F32)
-    quarter = count // 4
-    lower_keep = jnp.where((me != quarter) & (me != 3 * quarter), 1.0, 0.0)
-    upper_keep = jnp.where((me != quarter - 1) & (me != 3 * quarter - 1), 1.0, 0.0)
-    halo_e[pl.ds(0, BINS, stride=LON), :] = stage_a[pl.ds(0, BINS), :]
-    halo_e[pl.ds(LON - 1, BINS, stride=LON), :] = stage_b[pl.ds(0, BINS), :]
-    halo_n[pl.ds(0, BINS, stride=LON), :] = stage_a[pl.ds(18, BINS), :] * lower_keep
-    halo_n[pl.ds(LON - 1, BINS, stride=LON), :] = stage_b[pl.ds(18, BINS), :] * upper_keep
+    def unpack(recv, halo, lower, upper):
+        for index, lon, factor in ((0, 0, lower), (1, LON - 1, upper)):
+            stage_a[...] = recv[index].astype(F32)
+            front = stage_a[pl.ds(0, direct), :]
+            rest = stage_a[pl.ds(18, folded), :]
+            if factor is not None:
+                front, rest = front * factor, rest * factor
+            halo[pl.ds(lon, direct, stride=LON), :] = front
+            halo[pl.ds(direct * LON + lon, folded, stride=LON), :] = rest
+
+    for copy in e_lon:
+        copy.wait()
+    unpack(e_recv, halo_e, None, None)
 
     def advect_band(band, total):
         block = rows_of(e_ref, band)
@@ -269,8 +347,6 @@
         bands_16[band] = moved.reshape(BAND_ROWS, LAT).astype(BF16)
         return total + 0.1 * ratio(band + REACH) * jnp.sum(moved, axis=0)
 
-    part[...] = lax.fori_loop(0, BANDS, advect_band, jnp.zeros((8, LAT), F32))
-
     def band_copy(start, recv, index, to):
         return pltpu.make_async_remote_copy(
             src_ref=bands_16.at[pl.ds(start, REACH)],
@@ -283,14 +359,17 @@
 
     upward = band_copy(BANDS - REACH, low_halo, 0, lax.rem(spec + 1, specs))
     downward = band_copy(0, high_halo, 1, lax.rem(spec + specs - 1, specs))
+    total = lax.fori_loop(0, REACH, advect_band, jnp.zeros((8, LAT), F32))
+
+    @pl.when(spec > 0)
+    def _():
+        downward.start()
+
+    part[...] = lax.fori_loop(REACH, BANDS, advect_band, total)
 
     @pl.when(spec < specs - 1)
     def _():
         upward.start()
-
-    @pl.when(spec > 0)
-    def _():
-        downward.start()
 
     sums = []
     for i in range(1, specs):
@@ -307,6 +386,16 @@
     for copy in sums:
         copy.start()
 
+    pl.semaphore_wait(ring_sem, RING - 1)
+    tell(half_sem, {"grid": x_peer})
+
+    quarter = count // 4
+    lower_keep = jnp.where((me != quarter) & (me != 3 * quarter), 1.0, 0.0)
+    upper_keep = jnp.where((me != quarter - 1) & (me != 3 * quarter - 1), 1.0, 0.0)
+    for copy in n_lon:
+        copy.wait()
+    unpack(n_recv, halo_n, lower_keep, upper_keep)
+
     def advect_nest(band, carry):
         block = rows_of(n_ref, band)
         lon_step, lat_step = upwind(block, rows_of(halo_n, band))
@@ -319,6 +408,11 @@
 
     lax.fori_loop(0, BANDS, advect_nest, 0)
 
+    for copy in sums:
+        copy.wait()
+    whole = part[...] + parts[1] + parts[2] + parts[3]
+    mean = (whole + pltpu.roll(whole, 4, axis=0)) * MEAN_SCALE
+
     @pl.when(spec < specs - 1)
     def _():
         upward.wait_send()
@@ -341,6 +435,8 @@
     chunk = 6
 
     def nonlinear_band(band, carry):
+        loss = ratio(band + REACH)
+        inverse_loss = (1.0 / (1.0 + dissip_coef * loss * loss * mean))[None]
         for piece in range(PAIRS // chunk):
             base = 2 + piece * chunk
 
@@ -368,39 +464,31 @@
                 - 2.0 * ratio(band + REACH) * own
             )
             start = pl.multiple_of(band * BAND_ROWS + piece * chunk * 8, 8)
-            g_buf[pl.ds(start, chunk * 8), :] = total.reshape(chunk * 8, LAT)
+            g_buf[pl.ds(start, chunk * 8), :] = (total * inverse_loss).reshape(chunk * 8, LAT)
         return carry
 
-    lax.fori_loop(0, BANDS, nonlinear_band, 0)
-
-    for copy in sums:
-        copy.wait()
-    whole = part[...] + parts[1] + parts[2] + parts[3]
-    mean = (whole + pltpu.roll(whole, 4, axis=0)) * MEAN_SCALE
-
-    def damp_band(band, carry):
-        value = ratio(band + REACH)
-        inverse_loss = 1.0 / (1.0 + dissip_coef * value * value * mean)
-        start = pl.multiple_of(band * BAND_ROWS, 8)
-        result = rows_of(g_buf, band) * inverse_loss[None]
-        g_buf[pl.ds(start, BAND_ROWS), :] = result.reshape(BAND_ROWS, LAT)
-        return carry
-
-    lax.fori_loop(0, BANDS, damp_band, 0)
+    def column_copy(start, rows, index):
+        return pltpu.make_async_remote_copy(
+            src_ref=col_send.at[pl.ds(start, rows)],
+            dst_ref=col_recv.at[pl.ds(start, rows)],
+            send_sem=col_ssem.at[index],
+            recv_sem=col_rsem.at[index],
+            device_id={"grid": west},
+            device_id_type=MESH,
+        )
+
+    columns = [column_copy(0, FIRST_ROWS, 0), column_copy(FIRST_ROWS, EAST - FIRST_ROWS, 1)]
+    first_bands = FIRST_ROWS // ANGLES
     g_buf[pl.ds(ROWS, WIDTH * LON - ROWS), :] = jnp.zeros((WIDTH * LON - ROWS, LAT), F32)
-
-    col_send[...] = g_buf[pl.ds(0, WIDTH, stride=LON), :].astype(BF16)
-    column = pltpu.make_async_remote_copy(
-        src_ref=col_send,
-        dst_ref=col_recv,
-        send_sem=col_ssem,
-        recv_sem=col_rsem,
-        device_id={"grid": west},
-        device_id_type=MESH,
-    )
-    column.start()
-    g_copy = pltpu.make_async_copy(g_buf.at[pl.ds(0, ROWS)], g_out, out_sem.at[0])
-    g_copy.start()
+    col_recv[pl.ds(EAST, WIDTH - EAST), :] = jnp.zeros((WIDTH - EAST, LAT), BF16)
+    lax.fori_loop(0, first_bands, nonlinear_band, 0)
+    col_send[pl.ds(0, FIRST_ROWS), :] = g_buf[pl.ds(0, FIRST_ROWS, stride=LON), :].astype(BF16)
+    columns[0].start()
+    lax.fori_loop(first_bands, BANDS, nonlinear_band, 0)
+    col_send[pl.ds(FIRST_ROWS, EAST - FIRST_ROWS), :] = g_buf[
+        pl.ds(FIRST_ROWS * LON, EAST - FIRST_ROWS, stride=LON), :
+    ].astype(BF16)
+    columns[1].start()
 
     boundary = jnp.zeros((RIM, WIDTH), F32)
     for lon in range(LON):
@@ -408,7 +496,8 @@
         boundary += dot_nt(share_high[lon], high)
         boundary += dot_nt(share_high[lon], low)
         boundary += dot_nt(share_low[lon], high)
-    column.wait()
+    for copy in columns:
+        copy.wait()
     boundary += dot_nt(share_high[LON], col_recv[...])
     boundary += dot_nt(share_low[LON], col_recv[...])
     boundary = jnp.concatenate([boundary[:, :256], boundary[:, 256:] + facts[...]], axis=1)
@@ -423,8 +512,11 @@
     own_block = pltpu.make_async_copy(blocks.at[me], arrived.at[me], rim_recv)
     own_block.start()
 
-    def post(i, carry):
-        dest = lax.rem(me + i, count)
+    pl.semaphore_wait(half_sem, 1)
+    for z, x, y in far_first():
+        dest = place_of(
+            turned_by(z_part, z, RING), 1 - x_part if x else x_part, turned_by(y_part, y, RING)
+        )
         pltpu.make_async_remote_copy(
             src_ref=blocks.at[dest],
             dst_ref=arrived.at[me],
@@ -433,9 +525,7 @@
             device_id={"grid": dest},
             device_id_type=MESH,
         ).start()
-        return carry
-
-    lax.fori_loop(1, count, post, 0)
+    g_out[...] = g_buf[pl.ds(0, ROWS), :]
     others = blocks.at[pl.ds(0, count - 1)]
     pltpu.make_async_copy(others, others, rim_send).wait()
     pltpu.make_async_copy(arrived, arrived, rim_recv).wait()
@@ -462,11 +552,7 @@
     for lon in range(LON):
         lanes = slice(lon * LAT, (lon + 1) * LAT)
         held = nest[pl.ds(lon, BINS, stride=LON), :]
-        n_buf[pl.ds(lon, BINS, stride=LON), :] = held * remains[:, lanes] + gained[:BINS, lanes]
-    n_copy = pltpu.make_async_copy(n_buf, n_out, out_sem.at[1])
-    n_copy.start()
-    g_copy.wait()
-    n_copy.wait()
+        n_out[pl.ds(lon, BINS, stride=LON), :] = held * remains[:, lanes] + gained[:BINS, lanes]
 
 
 def per_device(
@@ -484,15 +570,28 @@
     global_next, nest_next = pl.pallas_call(
         body,
         out_shape=(flat, flat),
-        in_specs=[vmem] * 11 + [pl.BlockSpec(memory_space=pltpu.SMEM)],
-        out_specs=(pl.BlockSpec(memory_space=pl.ANY), pl.BlockSpec(memory_space=pl.ANY)),
+        in_specs=[pl.BlockSpec(memory_space=pltpu.HBM)] * 12,
+        out_specs=(vmem, vmem),
         scratch_shapes=[
+            pltpu.VMEM((ROWS, LAT), F32),
+            pltpu.VMEM((ROWS, LAT), F32),
+            pltpu.VMEM((LON, LAT), jnp.int32),
+            pltpu.VMEM((2, LON, LAT), F32),
+            pltpu.VMEM((2, RIM), jnp.int32),
+            pltpu.VMEM((1, RIM), jnp.int32),
+            pltpu.VMEM((1, RIM), jnp.int32),
+            pltpu.VMEM((3, RIM), F32),
+            pltpu.VMEM((BAND_ROWS, LAT), F32),
+            pltpu.VMEM((BAND_ROWS, LAT), F32),
+            pltpu.VMEM((8, LAT), F32),
+            pltpu.SMEM((128,), F32),
+            pltpu.VMEM((RIM, RIM), F32),
             pltpu.VMEM((PACKET, LAT), F32),
             pltpu.VMEM((PACKET, LAT), F32),
-            pltpu.VMEM((PACKET, LAT), BF16),
-            pltpu.VMEM((PACKET, LAT), BF16),
-            pltpu.VMEM((PACKET, LAT), BF16),
-            pltpu.VMEM((PACKET, LAT), BF16),
+            pltpu.VMEM((2, PACKET, LAT), BF16),
+            pltpu.VMEM((2, PACKET, LAT), BF16),
+            pltpu.VMEM((2, PACKET, LAT), BF16),
+            pltpu.VMEM((2, PACKET, LAT), BF16),
             pltpu.VMEM((ROWS, LAT), F32),
             pltpu.VMEM((ROWS, LAT), F32),
             pltpu.VMEM((BANDS + 2 * REACH, PAIRS + 4, 8, LAT), F32),
@@ -503,7 +602,6 @@
             pltpu.VMEM((PAIRS, 8, LAT), F32),
             pltpu.VMEM((ROWS, LAT), F32),
             pltpu.VMEM((WIDTH * LON, LAT), F32),
-            pltpu.VMEM((ROWS, LAT), F32),
             pltpu.VMEM((8, LAT), F32),
             pltpu.VMEM((4, 8, LAT), F32),
             pltpu.VMEM((WIDTH, LAT), BF16),
@@ -515,35 +613,42 @@
             pltpu.VMEM((count * 8, LAT), F32),
             pltpu.VMEM((count, 8, LAT), BF16),
             pltpu.VMEM((count, 8, LAT), BF16),
-            dma((2,)),
-            dma((2,)),
+            dma((12,)),
+            dma((4,)),
+            dma((4,)),
             dma((2,)),
             dma((2,)),
             dma((4,)),
             dma((4,)),
+            dma((2,)),
+            dma((2,)),
             dma,
             dma,
-            dma,
-            dma,
-            dma((2,)),
+            pltpu.SemaphoreType.REGULAR,
+            pltpu.SemaphoreType.REGULAR,
         ],
         compiler_params=pltpu.CompilerParams(
             collective_id=0, has_side_effects=True, vmem_limit_bytes=40 << 20
         ),
         name="wave_step",
     )(
-        energy.reshape(ROWS, LAT),
-        nest_energy.reshape(ROWS, LAT),
-        ocean_mask,
-        wind_field,
-        rim_cell,
-        rim_dest,
-        rim_target.reshape(1, RIM),
-        rim_weight,
-        jnp.asarray(cosine),
-        jnp.asarray(sine),
-        jnp.asarray(secant),
-        jnp.asarray(scalars),
+        *(
+            pltpu.with_memory_space_constraint(x, pltpu.HBM)
+            for x in (
+                energy.reshape(ROWS, LAT),
+                nest_energy.reshape(ROWS, LAT),
+                ocean_mask,
+                wind_field,
+                rim_cell.T,
+                rim_dest.T,
+                rim_target.reshape(1, RIM),
+                rim_weight.T,
+                jnp.asarray(cosine),
+                jnp.asarray(sine),
+                jnp.asarray(secant),
+                jnp.asarray(scalars),
+            )
+        )
     )
     shape = energy.shape
     return (global_next.reshape(shape), nest_next.reshape(shape))

time: 56.3 us -> 46.5 us (0.83)
  Pallas kernels: 49.1 us -> 43.5 us
  local copies, waits for them, and re-layouts: 5.91 us -> 1.68 us
    pallas_call x1, Pallas kernels: 49.1 us -> 43.5 us  [per_device(): pl.pallas_call(body, out_shape=(flat, flat), in_specs=[pl.BlockSpec(memor...]
    unnamed x29 -> x2, local copies, waits for them, and re-layouts: 5.91 us -> 1.68 us
where the time goes in v3:
time: 46.5 us; the launch traced here: 45.8 us
  Pallas kernels  43.5 us (94%)
  local copies, waits for them, and re-layouts  1.68 us (4%)
  between operations  0.64 us (1%)
    pallas_call x1, Pallas kernels, per_device(): pl.pallas_call(body, out_shape=(flat, flat), in_specs=[pl.BlockSpec(memor...  43.5 us
    unnamed x2, local copies, waits for them, and re-layouts  1.68 us

profile of v3, /device:TPU:1, one launch (start us, length us, event | category | flops | bytes accessed | tf_op | source)
XLA Modules:
  0.0 45.8 jit_solution(928942420984426025)
XLA Ops:
  0.6 43.5 %wave_step.1 = (f32[1296,128]{1,0:T(8,128)S(1)}, f32[1296,128]{1,0:T(8,128)S(1)}) custom-call(f32[1296,128]{1,0:T(8,128)} %bitcast.10, f32[1296,128]{1,0:T(8,128)} %bitcast.11, s32[4,128]{1,0:T(4,128)} %refs_2_.1, f32[2,4,128]{2,1,0:T(4,128)} %refs_3_.1, s32[2,128]{1,0:T(2,128)} %bitcast.13, s32[1,128]{1,0:T(1,128)} %bitcast.14, s32[1,128]{1,0:T(1,128)} %bitcast.15, ...), custom_call_target="tpu_custom_call" | custom-call | tf_op jit(solution)/shard_map/wave_step/pallas_call | solution.py:570
  44.1 0.8 %copy.16 = f32[9,36,4,128]{3,2,1,0:T(4,128)} copy(f32[9,36,4,128]{3,2,1,0:T(4,128)S(1)} %bitcast.9) | data formatting | bytes 1327104
  45.0 0.8 %copy.17 = f32[9,36,4,128]{3,2,1,0:T(4,128)} copy(f32[9,36,4,128]{3,2,1,0:T(4,128)S(1)} %bitcast.8) | data formatting | bytes 1327104

commit v4 on v3

--- a/solution.py
+++ b/solution.py
@@ -17,10 +17,11 @@
 ROWS = BINS * LON
 BAND_ROWS = ANGLES * LON
 PAIRS = BAND_ROWS // 8
-PACKET = 208
+PACKET = 192
 FIRST_ROWS = 144
 EAST = 336
 RING = 8
+SETTLE_LIMIT = 16 << 20
 WIDTH = 384
 FACT = BINS - 256
 MESH = pl.DeviceIdType.MESH
@@ -93,7 +94,8 @@
     sec_hbm,
     scalar_hbm,
     g_out,
-    n_out,
+    nest,
+    arrived,
     e_ref,
     n_ref,
     mask_ref,
@@ -121,7 +123,6 @@
     low_halo,
     high_halo,
     gain,
-    nest,
     g_buf,
     part,
     parts,
@@ -131,9 +132,7 @@
     share_low,
     hot,
     facts,
-    slot_rows,
     blocks,
-    arrived,
     in_sem,
     lon_send,
     lon_recv,
@@ -240,12 +239,10 @@
         copy.start()
     for peer in z_peers:
         tell(ring_sem, {"grid": peer})
+    for load in loads[2:]:
+        load.wait()
     loads[1].wait()
     pack(n_ref, n_send)
-    for copy in n_lon:
-        copy.start()
-    for load in loads[2:]:
-        load.wait()
 
     lane = lax.broadcasted_iota(jnp.int32, (RIM, LAT), 1)
     sub = lax.broadcasted_iota(jnp.int32, (RIM, LAT), 0)
@@ -273,17 +270,15 @@
     dest_row = dest_ref[...].astype(F32)
     same = dest_col == dest_row
     slot_row = jnp.sum(jnp.where(same & (sub < lane), 1.0, 0.0), axis=0, keepdims=True)
-    named = dest_row == sub.astype(F32)
-    for j in range(2):
-        hot[pl.ds(j * RIM, RIM), :] = jnp.where(named & (slot_row == float(j)), 1.0, 0.0).astype(BF16)
+    places = lax.broadcasted_iota(jnp.int32, (2 * RIM, LAT), 0)
+    named = (dest_row == (places >> 1).astype(F32)) & (slot_row == (places & 1).astype(F32))
+    hot[...] = jnp.where(named, 1.0, 0.0).astype(BF16)
     relax_high = relax.astype(BF16).astype(F32)
     fact = jnp.where(lane == FACT, (target_col >> 7).astype(F32), 0.0)
     fact = jnp.where(lane == FACT + 1, (target_col & 127).astype(F32), fact)
     fact = jnp.where(lane == FACT + 2, relax_high, fact)
     fact = jnp.where(lane == FACT + 3, relax - relax_high, fact)
     facts[...] = fact
-    slot_rows[...] = jnp.zeros_like(slot_rows)
-
     pair_shape = (PAIRS, 8, LAT)
     cosine = cos_ref[...].reshape(pair_shape)
     sine = sin_ref[...].reshape(pair_shape)
@@ -336,7 +331,10 @@
         copy.wait()
     unpack(e_recv, halo_e, None, None)
 
-    def advect_band(band, total):
+    backward = lax.rem(spec, 2) == 1
+
+    def advect_band(index, total):
+        band = jnp.where(backward, BANDS - 1 - index, index)
         block = rows_of(e_ref, band)
         lon_step, lat_step = upwind(block, rows_of(halo_e, band))
         speed = speed_coef * inverse(band + REACH)
@@ -361,13 +359,21 @@
     downward = band_copy(0, high_halo, 1, lax.rem(spec + specs - 1, specs))
     total = lax.fori_loop(0, REACH, advect_band, jnp.zeros((8, LAT), F32))
 
-    @pl.when(spec > 0)
+    @pl.when((spec > 0) & ~backward)
     def _():
         downward.start()
 
+    @pl.when((spec < specs - 1) & backward)
+    def _():
+        upward.start()
+
     part[...] = lax.fori_loop(REACH, BANDS, advect_band, total)
 
-    @pl.when(spec < specs - 1)
+    @pl.when((spec > 0) & backward)
+    def _():
+        downward.start()
+
+    @pl.when((spec < specs - 1) & ~backward)
     def _():
         upward.start()
 
@@ -389,24 +395,57 @@
     pl.semaphore_wait(ring_sem, RING - 1)
     tell(half_sem, {"grid": x_peer})
 
-    quarter = count // 4
-    lower_keep = jnp.where((me != quarter) & (me != 3 * quarter), 1.0, 0.0)
-    upper_keep = jnp.where((me != quarter - 1) & (me != 3 * quarter - 1), 1.0, 0.0)
     for copy in n_lon:
-        copy.wait()
-    unpack(n_recv, halo_n, lower_keep, upper_keep)
-
-    def advect_nest(band, carry):
-        block = rows_of(n_ref, band)
-        lon_step, lat_step = upwind(block, rows_of(halo_n, band))
-        speed = nest_speedup * speed_coef * inverse(band + REACH)
-        along_x = jnp.abs(rows_of(cos_ref, 0))
-        along_y = jnp.abs(rows_of(sin_ref, 0))
-        moved = block - speed * (along_x * lon_step + along_y * lat_step)
-        nest[pl.ds(pl.multiple_of(band * BAND_ROWS, 8), BAND_ROWS), :] = moved.reshape(BAND_ROWS, LAT)
-        return carry
-
-    lax.fori_loop(0, BANDS, advect_nest, 0)
+        copy.start()
+
+    chunk = 6
+
+    def product(centre, upper, lower):
+        return centre * (centre * (upper + lower) - 2.0 * upper * lower)
+
+    def own_terms(here, at, band):
+        terms = [product(here, at(odd, 2, (3 * s - 1) // 2), at(odd, -3, (-s - 1) // 2)) for s in (1, -1)]
+        return (-2.0 * nonlin_coef * ratio(band + REACH)) * (terms[0] + terms[1])
+
+    def below_terms(here, at, band):
+        terms = [product(at(odd, -2, (-3 * s - 1) // 2), here, at(even, -5, -2 * s)) for s in (1, -1)]
+        return (nonlin_coef * ratio(band + REACH - 2)) * (terms[0] + terms[1])
+
+    def above_terms(here, at, band):
+        terms = [product(at(odd, 3, (s - 1) // 2), at(even, 5, 2 * s), here) for s in (1, -1)]
+        return (nonlin_coef * ratio(band + REACH + 3)) * (terms[0] + terms[1])
+
+    def add_terms(begin, end, kinds, opening, damped):
+        def step(band, carry):
+            if damped:
+                loss = ratio(band + REACH)
+                inverse_loss = (1.0 / (1.0 + dissip_coef * loss * loss * damped[0]))[None]
+            for piece in range(PAIRS // chunk):
+                base = 2 + piece * chunk
+
+                def at(ref, offset, turn):
+                    return ref[band + REACH + offset, pl.ds(base + turn, chunk)]
+
+                here = at(even, 0, 0)
+                rows = pl.ds(pl.multiple_of(band * BAND_ROWS + piece * chunk * 8, 8), chunk * 8)
+                if opening:
+                    total = here * (1.0 + ratio(band + REACH) * gain[pl.ds(piece * chunk, chunk)])
+                else:
+                    total = g_buf[rows, :].reshape(chunk, 8, LAT)
+                for kind in kinds:
+                    total += kind(here, at, band)
+                if damped:
+                    total *= inverse_loss
+                g_buf[rows, :] = total.reshape(chunk * 8, LAT)
+            return carry
+
+        lax.fori_loop(begin, end, step, 0)
+
+    add_terms(0, 3, (above_terms,), True, ())
+    add_terms(3, 4, (own_terms, above_terms), True, ())
+    add_terms(4, 5, (own_terms,), True, ())
+    add_terms(5, 7, (own_terms, below_terms), True, ())
+    add_terms(7, 9, (below_terms,), True, ())
 
     for copy in sums:
         copy.wait()
@@ -431,41 +470,6 @@
         return carry
 
     lax.fori_loop(0, REACH, halo_bands, 0)
-
-    chunk = 6
-
-    def nonlinear_band(band, carry):
-        loss = ratio(band + REACH)
-        inverse_loss = (1.0 / (1.0 + dissip_coef * loss * loss * mean))[None]
-        for piece in range(PAIRS // chunk):
-            base = 2 + piece * chunk
-
-            def at(ref, offset, turn):
-                return ref[band + REACH + offset, pl.ds(base + turn, chunk)]
-
-            here = at(even, 0, 0)
-            total = here * (1.0 + ratio(band + REACH) * gain[pl.ds(piece * chunk, chunk)])
-
-            def product(centre, upper, lower):
-                return centre * (centre * (upper + lower) - 2.0 * upper * lower)
-
-            own = 0.0
-            below = 0.0
-            above = 0.0
-            for s in (1, -1):
-                own += product(
-                    here, at(odd, 2, (3 * s - 1) // 2), at(odd, -3, (-s - 1) // 2)
-                )
-                below += product(at(odd, -2, (-3 * s - 1) // 2), here, at(even, -5, -2 * s))
-                above += product(at(odd, 3, (s - 1) // 2), at(even, 5, 2 * s), here)
-            total += nonlin_coef * (
-                ratio(band + REACH - 2) * below
-                + ratio(band + REACH + 3) * above
-                - 2.0 * ratio(band + REACH) * own
-            )
-            start = pl.multiple_of(band * BAND_ROWS + piece * chunk * 8, 8)
-            g_buf[pl.ds(start, chunk * 8), :] = (total * inverse_loss).reshape(chunk * 8, LAT)
-        return carry
 
     def column_copy(start, rows, index):
         return pltpu.make_async_remote_copy(
@@ -478,13 +482,15 @@
         )
 
     columns = [column_copy(0, FIRST_ROWS, 0), column_copy(FIRST_ROWS, EAST - FIRST_ROWS, 1)]
-    first_bands = FIRST_ROWS // ANGLES
     g_buf[pl.ds(ROWS, WIDTH * LON - ROWS), :] = jnp.zeros((WIDTH * LON - ROWS, LAT), F32)
     col_recv[pl.ds(EAST, WIDTH - EAST), :] = jnp.zeros((WIDTH - EAST, LAT), BF16)
-    lax.fori_loop(0, first_bands, nonlinear_band, 0)
+    add_terms(0, 3, (own_terms, below_terms), False, (mean,))
+    add_terms(3, 4, (below_terms,), False, (mean,))
     col_send[pl.ds(0, FIRST_ROWS), :] = g_buf[pl.ds(0, FIRST_ROWS, stride=LON), :].astype(BF16)
     columns[0].start()
-    lax.fori_loop(first_bands, BANDS, nonlinear_band, 0)
+    add_terms(4, 5, (below_terms, above_terms), False, (mean,))
+    add_terms(5, 7, (above_terms,), False, (mean,))
+    add_terms(7, 9, (own_terms, above_terms), False, (mean,))
     col_send[pl.ds(FIRST_ROWS, EAST - FIRST_ROWS), :] = g_buf[
         pl.ds(FIRST_ROWS * LON, EAST - FIRST_ROWS, stride=LON), :
     ].astype(BF16)
@@ -502,14 +508,11 @@
     boundary += dot_nt(share_low[LON], col_recv[...])
     boundary = jnp.concatenate([boundary[:, :256], boundary[:, 256:] + facts[...]], axis=1)
     packed = jnp.dot(hot[...], boundary.astype(BF16), preferred_element_type=F32)
-    for j in range(2):
-        for c in range(3):
-            slot_rows[pl.ds(j * 3 + c, RIM, stride=8), :] = packed[
-                j * RIM : (j + 1) * RIM, c * LAT : (c + 1) * LAT
-            ]
-    blocks[...] = slot_rows[...].reshape(count, 8, LAT).astype(BF16)
-
-    own_block = pltpu.make_async_copy(blocks.at[me], arrived.at[me], rim_recv)
+    for c in range(3):
+        lanes = packed[:, c * LAT : (c + 1) * LAT].astype(BF16)
+        blocks[c] = lanes.reshape(count, 2, LAT)
+
+    own_block = pltpu.make_async_copy(blocks.at[:, me], arrived.at[:, me], rim_recv)
     own_block.start()
 
     pl.semaphore_wait(half_sem, 1)
@@ -518,27 +521,44 @@
             turned_by(z_part, z, RING), 1 - x_part if x else x_part, turned_by(y_part, y, RING)
         )
         pltpu.make_async_remote_copy(
-            src_ref=blocks.at[dest],
-            dst_ref=arrived.at[me],
+            src_ref=blocks.at[:, dest],
+            dst_ref=arrived.at[:, me],
             send_sem=rim_send,
             recv_sem=rim_recv,
             device_id={"grid": dest},
             device_id_type=MESH,
         ).start()
     g_out[...] = g_buf[pl.ds(0, ROWS), :]
-    others = blocks.at[pl.ds(0, count - 1)]
+    quarter = count // 4
+    lower_keep = jnp.where((me != quarter) & (me != 3 * quarter), 1.0, 0.0)
+    upper_keep = jnp.where((me != quarter - 1) & (me != 3 * quarter - 1), 1.0, 0.0)
+    for copy in n_lon:
+        copy.wait()
+    unpack(n_recv, halo_n, lower_keep, upper_keep)
+
+    def advect_nest(band, carry):
+        block = rows_of(n_ref, band)
+        lon_step, lat_step = upwind(block, rows_of(halo_n, band))
+        speed = nest_speedup * speed_coef * inverse(band + REACH)
+        along_x = jnp.abs(rows_of(cos_ref, 0))
+        along_y = jnp.abs(rows_of(sin_ref, 0))
+        moved = block - speed * (along_x * lon_step + along_y * lat_step)
+        nest[pl.ds(pl.multiple_of(band * BAND_ROWS, 8), BAND_ROWS), :] = moved.reshape(BAND_ROWS, LAT)
+        return carry
+
+    lax.fori_loop(0, BANDS, advect_nest, 0)
+
+    others = blocks.at[:, pl.ds(0, count - 1)]
     pltpu.make_async_copy(others, others, rim_send).wait()
     pltpu.make_async_copy(arrived, arrived, rim_recv).wait()
 
-    slot_rows[...] = arrived[...].astype(F32).reshape(count * 8, LAT)
-    halves = []
-    for j in range(2):
-        halves.append(
-            jnp.concatenate(
-                [slot_rows[pl.ds(j * 3 + c, RIM, stride=8), :] for c in range(3)], axis=1
-            )
-        )
-    spectra = jnp.concatenate(halves, axis=0)
+
+def settle(arrived, nest, g_next, g_out, n_out, n_buf, out_sem):
+    g_copy = pltpu.make_async_copy(g_next, g_out, out_sem.at[0])
+    g_copy.start()
+    spectra = jnp.concatenate(
+        [arrived[c].reshape(2 * RIM, LAT).astype(F32) for c in range(3)], axis=1
+    )
     told = spectra[:, 256:]
     cell = told[:, FACT : FACT + 1] * float(LAT) + told[:, FACT + 1 : FACT + 2]
     cells = lax.broadcasted_iota(jnp.int32, (2 * RIM, LON * LAT), 1).astype(F32)
@@ -552,7 +572,11 @@
     for lon in range(LON):
         lanes = slice(lon * LAT, (lon + 1) * LAT)
         held = nest[pl.ds(lon, BINS, stride=LON), :]
-        n_out[pl.ds(lon, BINS, stride=LON), :] = held * remains[:, lanes] + gained[:BINS, lanes]
+        n_buf[pl.ds(lon, BINS, stride=LON), :] = held * remains[:, lanes] + gained[:BINS, lanes]
+    n_copy = pltpu.make_async_copy(n_buf, n_out, out_sem.at[1])
+    n_copy.start()
+    g_copy.wait()
+    n_copy.wait()
 
 
 def per_device(
@@ -567,11 +591,11 @@
     def body(*refs):
         kernel(count, *refs)
 
-    global_next, nest_next = pl.pallas_call(
+    global_rows, nest_rows, arrived = pl.pallas_call(
         body,
-        out_shape=(flat, flat),
+        out_shape=(flat, flat, jax.ShapeDtypeStruct((3, count, 2, LAT), BF16)),
         in_specs=[pl.BlockSpec(memory_space=pltpu.HBM)] * 12,
-        out_specs=(vmem, vmem),
+        out_specs=(vmem, vmem, vmem),
         scratch_shapes=[
             pltpu.VMEM((ROWS, LAT), F32),
             pltpu.VMEM((ROWS, LAT), F32),
@@ -600,7 +624,6 @@
             pltpu.VMEM((REACH, BAND_ROWS, LAT), BF16),
             pltpu.VMEM((REACH, BAND_ROWS, LAT), BF16),
             pltpu.VMEM((PAIRS, 8, LAT), F32),
-            pltpu.VMEM((ROWS, LAT), F32),
             pltpu.VMEM((WIDTH * LON, LAT), F32),
             pltpu.VMEM((8, LAT), F32),
             pltpu.VMEM((4, 8, LAT), F32),
@@ -610,9 +633,7 @@
             pltpu.VMEM((LON + 1, RIM, LAT), BF16),
             pltpu.VMEM((2 * RIM, RIM), BF16),
             pltpu.VMEM((RIM, LAT), F32),
-            pltpu.VMEM((count * 8, LAT), F32),
-            pltpu.VMEM((count, 8, LAT), BF16),
-            pltpu.VMEM((count, 8, LAT), BF16),
+            pltpu.VMEM((3, count, 2, LAT), BF16),
             dma((12,)),
             dma((4,)),
             dma((4,)),
@@ -650,6 +671,19 @@
             )
         )
     )
+    hbm = pl.BlockSpec(memory_space=pl.ANY)
+    global_next, nest_next = pl.pallas_call(
+        settle,
+        out_shape=(flat, flat),
+        in_specs=[vmem] * 3,
+        out_specs=(hbm, hbm),
+        scratch_shapes=[
+            pltpu.VMEM((ROWS, LAT), F32),
+            dma((2,)),
+        ],
+        compiler_params=pltpu.CompilerParams(vmem_limit_bytes=SETTLE_LIMIT),
+        name="settle",
+    )(arrived, nest_rows, global_rows)
     shape = energy.shape
     return (global_next.reshape(shape), nest_next.reshape(shape))
 

time: 46.5 us -> 44.7 us (0.961); the launches traced: 45.8 us -> 44.5 us
  local copies, waits for them, and re-layouts: 1.68 us -> 0 us
    unnamed x2 -> x0, local copies, waits for them, and re-layouts: 1.68 us -> none
    pallas_call x1 -> x2, Pallas kernels: 43.5 us -> 43.9 us  [the longest x1 42.4 us: per_device(): pl.pallas_call(body, out_shape=(flat, flat, jax.ShapeDtypeStruct((3, coun...]
where the time goes in v4:
time: 44.7 us; the launch traced here: 44.5 us
  Pallas kernels  43.9 us (98%)
  between operations  0.64 us (1%)
    pallas_call x1, Pallas kernels, per_device(): pl.pallas_call(body, out_shape=(flat, flat, jax.ShapeDtypeStruct((3, coun...  42.4 us
    pallas_call x1, Pallas kernels, per_device(): pl.pallas_call(settle, out_shape=(flat, flat), in_specs=[vmem] * 3, out_s...  1.5 us

profile of v4, /device:TPU:1, one launch (start us, length us, event | category | flops | bytes accessed | tf_op | source)
XLA Modules:
  0.0 44.5 jit_solution(9050640073499108030)
XLA Ops:
  0.6 42.4 %wave_step.1 = (f32[1296,128]{1,0:T(8,128)S(1)}, f32[1296,128]{1,0:T(8,128)S(1)}, bf16[3,128,2,128]{3,2,1,0:T(2,128)(2,1)S(1)}) custom-call(f32[1296,128]{1,0:T(8,128)} %bitcast.8, f32[1296,128]{1,0:T(8,128)} %bitcast.9, s32[4,128]{1,0:T(4,128)} %refs_2_.1, f32[2,4,128]{2,1,0:T(4,128)} %refs_3_.1, s32[2,128]{1,0:T(2,128)} %bitcast.11, s32[1,128]{1,0:T(1,128)} %bitcast.12, ...), custom_call_target="tpu_custom_call" | custom-call | tf_op jit(solution)/shard_map/wave_step/pallas_call | solution.py:594
  43.0 1.5 %settle.1 = (f32[1296,128]{1,0:T(8,128)}, f32[1296,128]{1,0:T(8,128)}) custom-call(bf16[3,128,2,128]{3,2,1,0:T(2,128)(2,1)S(1)} %get-tuple-element.7.arrived, f32[1296,128]{1,0:T(8,128)S(1)} %get-tuple-element.8.nest, f32[1296,128]{1,0:T(8,128)S(1)} %get-tuple-element.9.g_next), custom_call_target="tpu_custom_call" | custom-call | tf_op jit(solution)/shard_map/settle/pallas_call | solution.py:675

commit v5 on v4

--- a/solution.py
+++ b/solution.py
@@ -144,6 +144,7 @@
     col_rsem,
     rim_send,
     rim_recv,
+    near_sem,
     ring_sem,
     half_sem,
 ):
@@ -194,9 +195,10 @@
         tell(barrier, {"spec": lax.rem(spec + i, specs)})
     z_peers = [place_of(turned_by(z_part, i, RING), x_part, y_part) for i in range(1, RING)]
     x_peer = place_of(z_part, 1 - x_part, y_part)
-    for i in range(1, RING):
-        tell(barrier, {"grid": place_of(z_part, x_part, turned_by(y_part, i, RING))})
-    for peer in z_peers:
+    near = (1, RING - 1, 2, RING - 2)
+    y_near = [place_of(z_part, x_part, turned_by(y_part, i, RING)) for i in near]
+    z_near = [z_peers[i - 1] for i in near]
+    for peer in y_near + z_near:
         tell(barrier, {"grid": peer})
     tell(barrier, {"grid": x_peer})
     for load in loads[2:]:
@@ -218,7 +220,7 @@
 
     loads[0].wait()
     pack(e_ref, e_send)
-    pl.semaphore_wait(barrier, 2 + specs - 1 + 2 * (RING - 1) + 1)
+    pl.semaphore_wait(barrier, 2 + specs - 1 + 2 * len(near) + 1)
 
     def lon_copies(send, recv, base):
         return [
@@ -237,8 +239,8 @@
     n_lon = lon_copies(n_send, n_recv, 2)
     for copy in e_lon:
         copy.start()
-    for peer in z_peers:
-        tell(ring_sem, {"grid": peer})
+    for peer in y_near[2:] + z_near[2:]:
+        tell(near_sem, {"grid": peer})
     for load in loads[2:]:
         load.wait()
     loads[1].wait()
@@ -328,7 +330,7 @@
             halo[pl.ds(direct * LON + lon, folded, stride=LON), :] = rest
 
     for copy in e_lon:
-        copy.wait()
+        copy.wait_recv()
     unpack(e_recv, halo_e, None, None)
 
     backward = lax.rem(spec, 2) == 1
@@ -392,8 +394,9 @@
     for copy in sums:
         copy.start()
 
-    pl.semaphore_wait(ring_sem, RING - 1)
-    tell(half_sem, {"grid": x_peer})
+    pl.semaphore_wait(near_sem, 4)
+    for peer in z_peers:
+        tell(ring_sem, {"grid": peer})
 
     for copy in n_lon:
         copy.start()
@@ -448,19 +451,17 @@
     add_terms(7, 9, (below_terms,), True, ())
 
     for copy in sums:
-        copy.wait()
+        copy.wait_recv()
     whole = part[...] + parts[1] + parts[2] + parts[3]
     mean = (whole + pltpu.roll(whole, 4, axis=0)) * MEAN_SCALE
 
     @pl.when(spec < specs - 1)
     def _():
-        upward.wait_send()
         downward.wait_recv()
 
     @pl.when(spec > 0)
     def _():
         upward.wait_recv()
-        downward.wait_send()
 
     def halo_bands(band, carry):
         low = low_halo[band].astype(F32).reshape(pair_shape)
@@ -488,6 +489,8 @@
     add_terms(3, 4, (below_terms,), False, (mean,))
     col_send[pl.ds(0, FIRST_ROWS), :] = g_buf[pl.ds(0, FIRST_ROWS, stride=LON), :].astype(BF16)
     columns[0].start()
+    pl.semaphore_wait(ring_sem, RING - 1)
+    tell(half_sem, {"grid": x_peer})
     add_terms(4, 5, (below_terms, above_terms), False, (mean,))
     add_terms(5, 7, (above_terms,), False, (mean,))
     add_terms(7, 9, (own_terms, above_terms), False, (mean,))
@@ -503,7 +506,7 @@
         boundary += dot_nt(share_high[lon], low)
         boundary += dot_nt(share_low[lon], high)
     for copy in columns:
-        copy.wait()
+        copy.wait_recv()
     boundary += dot_nt(share_high[LON], col_recv[...])
     boundary += dot_nt(share_low[LON], col_recv[...])
     boundary = jnp.concatenate([boundary[:, :256], boundary[:, 256:] + facts[...]], axis=1)
@@ -533,7 +536,7 @@
     lower_keep = jnp.where((me != quarter) & (me != 3 * quarter), 1.0, 0.0)
     upper_keep = jnp.where((me != quarter - 1) & (me != 3 * quarter - 1), 1.0, 0.0)
     for copy in n_lon:
-        copy.wait()
+        copy.wait_recv()
     unpack(n_recv, halo_n, lower_keep, upper_keep)
 
     def advect_nest(band, carry):
@@ -547,6 +550,17 @@
         return carry
 
     lax.fori_loop(0, BANDS, advect_nest, 0)
+
+    for copy in e_lon + n_lon + sums + columns:
+        copy.wait_send()
+
+    @pl.when(spec < specs - 1)
+    def _():
+        upward.wait_send()
+
+    @pl.when(spec > 0)
+    def _():
+        downward.wait_send()
 
     others = blocks.at[:, pl.ds(0, count - 1)]
     pltpu.make_async_copy(others, others, rim_send).wait()
@@ -647,6 +661,7 @@
             dma,
             pltpu.SemaphoreType.REGULAR,
             pltpu.SemaphoreType.REGULAR,
+            pltpu.SemaphoreType.REGULAR,
         ],
         compiler_params=pltpu.CompilerParams(
             collective_id=0, has_side_effects=True, vmem_limit_bytes=40 << 20

time: 44.7 us -> 44.1 us (0.987)
  Pallas kernels: 43.9 us -> 42.9 us
    pallas_call x1, Pallas kernels: 42.4 us -> 41.4 us  [per_device(): pl.pallas_call(body, out_shape=(flat, flat, jax.ShapeDtypeStruct((3, coun...]
where the time goes in v5:
time: 44.1 us; the launch traced here: 43.5 us
  Pallas kernels  42.9 us (97%)
  between operations  0.64 us (1%)
    pallas_call x1, Pallas kernels, per_device(): pl.pallas_call(body, out_shape=(flat, flat, jax.ShapeDtypeStruct((3, coun...  41.4 us
    pallas_call x1, Pallas kernels, per_device(): pl.pallas_call(settle, out_shape=(flat, flat), in_specs=[vmem] * 3, out_s...  1.5 us

profile of v5, /device:TPU:1, one launch (start us, length us, event | category | flops | bytes accessed | tf_op | source)
XLA Modules:
  0.0 43.5 jit_solution(6173766612329962082)
XLA Ops:
  0.6 41.4 %wave_step.1 = (f32[1296,128]{1,0:T(8,128)S(1)}, f32[1296,128]{1,0:T(8,128)S(1)}, bf16[3,128,2,128]{3,2,1,0:T(2,128)(2,1)S(1)}) custom-call(f32[1296,128]{1,0:T(8,128)} %bitcast.8, f32[1296,128]{1,0:T(8,128)} %bitcast.9, s32[4,128]{1,0:T(4,128)} %refs_2_.1, f32[2,4,128]{2,1,0:T(4,128)} %refs_3_.1, s32[2,128]{1,0:T(2,128)} %bitcast.11, s32[1,128]{1,0:T(1,128)} %bitcast.12, ...), custom_call_target="tpu_custom_call" | custom-call | tf_op jit(solution)/shard_map/wave_step/pallas_call | solution.py:608
  42.0 1.5 %settle.1 = (f32[1296,128]{1,0:T(8,128)}, f32[1296,128]{1,0:T(8,128)}) custom-call(bf16[3,128,2,128]{3,2,1,0:T(2,128)(2,1)S(1)} %get-tuple-element.7.arrived, f32[1296,128]{1,0:T(8,128)S(1)} %get-tuple-element.8.nest, f32[1296,128]{1,0:T(8,128)S(1)} %get-tuple-element.9.g_next), custom_call_target="tpu_custom_call" | custom-call | tf_op jit(solution)/shard_map/settle/pallas_call | solution.py:690

commit v6 on v5

--- a/solution.py
+++ b/solution.py
@@ -130,7 +130,6 @@
     col_recv,
     share_high,
     share_low,
-    hot,
     facts,
     blocks,
     in_sem,
@@ -262,25 +261,28 @@
     ny = rim_cols[:, 5:6]
     relax = rim_cols[:, 6:7]
     row_share = jnp.where(lane == row, 1.0 - ny, jnp.where(lane == row + 1, ny, 0.0))
+    shares = []
     for lon in range(LON + 1):
         col_share = jnp.where(
             local_col == lon, 1.0 - ex, jnp.where(local_col == lon - 1, ex, 0.0)
         )
         high, low = split_16(col_share * row_share)
-        share_high[lon] = high
-        share_low[lon] = low
+        shares.append((high, low))
     dest_row = dest_ref[...].astype(F32)
     same = dest_col == dest_row
     slot_row = jnp.sum(jnp.where(same & (sub < lane), 1.0, 0.0), axis=0, keepdims=True)
     places = lax.broadcasted_iota(jnp.int32, (2 * RIM, LAT), 0)
     named = (dest_row == (places >> 1).astype(F32)) & (slot_row == (places & 1).astype(F32))
-    hot[...] = jnp.where(named, 1.0, 0.0).astype(BF16)
+    hot = jnp.where(named, 1.0, 0.0).astype(BF16)
     relax_high = relax.astype(BF16).astype(F32)
     fact = jnp.where(lane == FACT, (target_col >> 7).astype(F32), 0.0)
     fact = jnp.where(lane == FACT + 1, (target_col & 127).astype(F32), fact)
     fact = jnp.where(lane == FACT + 2, relax_high, fact)
     fact = jnp.where(lane == FACT + 3, relax - relax_high, fact)
-    facts[...] = fact
+    facts[...] = jnp.dot(hot, fact.astype(BF16), preferred_element_type=F32)
+    for lon, (high, low) in enumerate(shares):
+        share_high[lon] = jnp.dot(hot, high, preferred_element_type=F32).astype(BF16)
+        share_low[lon] = jnp.dot(hot, low, preferred_element_type=F32).astype(BF16)
     pair_shape = (PAIRS, 8, LAT)
     cosine = cos_ref[...].reshape(pair_shape)
     sine = sin_ref[...].reshape(pair_shape)
@@ -332,6 +334,9 @@
     for copy in e_lon:
         copy.wait_recv()
     unpack(e_recv, halo_e, None, None)
+    pl.semaphore_wait(near_sem, 4)
+    for peer in z_peers:
+        tell(ring_sem, {"grid": peer})
 
     backward = lax.rem(spec, 2) == 1
 
@@ -394,9 +399,6 @@
     for copy in sums:
         copy.start()
 
-    pl.semaphore_wait(near_sem, 4)
-    for peer in z_peers:
-        tell(ring_sem, {"grid": peer})
 
     for copy in n_lon:
         copy.start()
@@ -489,8 +491,6 @@
     add_terms(3, 4, (below_terms,), False, (mean,))
     col_send[pl.ds(0, FIRST_ROWS), :] = g_buf[pl.ds(0, FIRST_ROWS, stride=LON), :].astype(BF16)
     columns[0].start()
-    pl.semaphore_wait(ring_sem, RING - 1)
-    tell(half_sem, {"grid": x_peer})
     add_terms(4, 5, (below_terms, above_terms), False, (mean,))
     add_terms(5, 7, (above_terms,), False, (mean,))
     add_terms(7, 9, (own_terms, above_terms), False, (mean,))
@@ -498,21 +498,24 @@
         pl.ds(FIRST_ROWS * LON, EAST - FIRST_ROWS, stride=LON), :
     ].astype(BF16)
     columns[1].start()
-
-    boundary = jnp.zeros((RIM, WIDTH), F32)
+    pl.semaphore_wait(ring_sem, RING - 1)
+    tell(half_sem, {"grid": x_peer})
+
+    packed = jnp.zeros((2 * RIM, WIDTH), F32)
     for lon in range(LON):
         high, low = split_16(g_buf[pl.ds(lon, WIDTH, stride=LON), :])
-        boundary += dot_nt(share_high[lon], high)
-        boundary += dot_nt(share_high[lon], low)
-        boundary += dot_nt(share_low[lon], high)
+        packed += dot_nt(share_high[lon], high)
+        packed += dot_nt(share_high[lon], low)
+        packed += dot_nt(share_low[lon], high)
     for copy in columns:
         copy.wait_recv()
-    boundary += dot_nt(share_high[LON], col_recv[...])
-    boundary += dot_nt(share_low[LON], col_recv[...])
-    boundary = jnp.concatenate([boundary[:, :256], boundary[:, 256:] + facts[...]], axis=1)
-    packed = jnp.dot(hot[...], boundary.astype(BF16), preferred_element_type=F32)
+    packed += dot_nt(share_high[LON], col_recv[...])
+    packed += dot_nt(share_low[LON], col_recv[...])
     for c in range(3):
-        lanes = packed[:, c * LAT : (c + 1) * LAT].astype(BF16)
+        lanes = packed[:, c * LAT : (c + 1) * LAT]
+        if c == 2:
+            lanes += facts[...]
+        lanes = lanes.astype(BF16)
         blocks[c] = lanes.reshape(count, 2, LAT)
 
     own_block = pltpu.make_async_copy(blocks.at[:, me], arrived.at[:, me], rim_recv)
@@ -570,17 +573,15 @@
 def settle(arrived, nest, g_next, g_out, n_out, n_buf, out_sem):
     g_copy = pltpu.make_async_copy(g_next, g_out, out_sem.at[0])
     g_copy.start()
-    spectra = jnp.concatenate(
-        [arrived[c].reshape(2 * RIM, LAT).astype(F32) for c in range(3)], axis=1
-    )
-    told = spectra[:, 256:]
+    spectra = jnp.concatenate([arrived[c].reshape(2 * RIM, LAT) for c in range(3)], axis=1)
+    told = spectra[:, 256:].astype(F32)
     cell = told[:, FACT : FACT + 1] * float(LAT) + told[:, FACT + 1 : FACT + 2]
     cells = lax.broadcasted_iota(jnp.int32, (2 * RIM, LON * LAT), 1).astype(F32)
     hit = cell == cells
     rate_high = jnp.where(hit, told[:, FACT + 2 : FACT + 3], 0.0)
     rate_low = jnp.where(hit, told[:, FACT + 3 : FACT + 4], 0.0)
     remains = 1.0 - jnp.sum(rate_high + rate_low, axis=0, keepdims=True)
-    turned = spectra.T.astype(BF16)
+    turned = spectra.T
     gained = jnp.dot(turned, rate_high.astype(BF16), preferred_element_type=F32)
     gained += jnp.dot(turned, rate_low.astype(BF16), preferred_element_type=F32)
     for lon in range(LON):
@@ -643,10 +644,9 @@
             pltpu.VMEM((4, 8, LAT), F32),
             pltpu.VMEM((WIDTH, LAT), BF16),
             pltpu.VMEM((WIDTH, LAT), BF16),
-            pltpu.VMEM((LON + 1, RIM, LAT), BF16),
-            pltpu.VMEM((LON + 1, RIM, LAT), BF16),
-            pltpu.VMEM((2 * RIM, RIM), BF16),
-            pltpu.VMEM((RIM, LAT), F32),
+            pltpu.VMEM((LON + 1, 2 * RIM, LAT), BF16),
+            pltpu.VMEM((LON + 1, 2 * RIM, LAT), BF16),
+            pltpu.VMEM((2 * RIM, LAT), F32),
             pltpu.VMEM((3, count, 2, LAT), BF16),
             dma((12,)),
             dma((4,)),

time: 44.1 us -> 43.8 us (level)
  no operation moved by 1% of the time
where the time goes in v6:
time: 43.8 us; the launch traced here: 43.6 us
  Pallas kernels  43 us (98%)
  between operations  0.64 us (1%)
    pallas_call x1, Pallas kernels, per_device(): pl.pallas_call(body, out_shape=(flat, flat, jax.ShapeDtypeStruct((3, coun...  41.5 us
    pallas_call x1, Pallas kernels, per_device(): pl.pallas_call(settle, out_shape=(flat, flat), in_specs=[vmem] * 3, out_s...  1.45 us

profile of v6, /device:TPU:1, one launch (start us, length us, event | category | flops | bytes accessed | tf_op | source)
XLA Modules:
  0.0 43.6 jit_solution(4207249317841559327)
XLA Ops:
  0.6 41.5 %wave_step.1 = (f32[1296,128]{1,0:T(8,128)S(1)}, f32[1296,128]{1,0:T(8,128)S(1)}, bf16[3,128,2,128]{3,2,1,0:T(2,128)(2,1)S(1)}) custom-call(f32[1296,128]{1,0:T(8,128)} %bitcast.8, f32[1296,128]{1,0:T(8,128)} %bitcast.9, s32[4,128]{1,0:T(4,128)} %refs_2_.1, f32[2,4,128]{2,1,0:T(4,128)} %refs_3_.1, s32[2,128]{1,0:T(2,128)} %bitcast.11, s32[1,128]{1,0:T(1,128)} %bitcast.12, ...), custom_call_target="tpu_custom_call" | custom-call | tf_op jit(solution)/shard_map/wave_step/pallas_call | solution.py:609
  42.2 1.4 %settle.1 = (f32[1296,128]{1,0:T(8,128)}, f32[1296,128]{1,0:T(8,128)}) custom-call(bf16[3,128,2,128]{3,2,1,0:T(2,128)(2,1)S(1)} %get-tuple-element.7.arrived, f32[1296,128]{1,0:T(8,128)S(1)} %get-tuple-element.8.nest, f32[1296,128]{1,0:T(8,128)S(1)} %get-tuple-element.9.g_next), custom_call_target="tpu_custom_call" | custom-call | tf_op jit(solution)/shard_map/settle/pallas_call | solution.py:690

commit v7 on v6

--- a/solution.py
+++ b/solution.py
@@ -23,6 +23,7 @@
 RING = 8
 SETTLE_LIMIT = 16 << 20
 WIDTH = 384
+ROOM = 8 * -(-BINS // 8) * LON
 FACT = BINS - 256
 MESH = pl.DeviceIdType.MESH
 F32 = jnp.float32
@@ -588,7 +589,7 @@
         lanes = slice(lon * LAT, (lon + 1) * LAT)
         held = nest[pl.ds(lon, BINS, stride=LON), :]
         n_buf[pl.ds(lon, BINS, stride=LON), :] = held * remains[:, lanes] + gained[:BINS, lanes]
-    n_copy = pltpu.make_async_copy(n_buf, n_out, out_sem.at[1])
+    n_copy = pltpu.make_async_copy(n_buf.at[pl.ds(0, ROWS)], n_out, out_sem.at[1])
     n_copy.start()
     g_copy.wait()
     n_copy.wait()
@@ -608,7 +609,7 @@
 
     global_rows, nest_rows, arrived = pl.pallas_call(
         body,
-        out_shape=(flat, flat, jax.ShapeDtypeStruct((3, count, 2, LAT), BF16)),
+        out_shape=(flat, jax.ShapeDtypeStruct((ROOM, LAT), F32), jax.ShapeDtypeStruct((3, count, 2, LAT), BF16)),
         in_specs=[pl.BlockSpec(memory_space=pltpu.HBM)] * 12,
         out_specs=(vmem, vmem, vmem),
         scratch_shapes=[
@@ -693,7 +694,7 @@
         in_specs=[vmem] * 3,
         out_specs=(hbm, hbm),
         scratch_shapes=[
-            pltpu.VMEM((ROWS, LAT), F32),
+            pltpu.VMEM((ROOM, LAT), F32),
             dma((2,)),
         ],
         compiler_params=pltpu.CompilerParams(vmem_limit_bytes=SETTLE_LIMIT),

time: 43.8 us -> 43.8 us (level)
  no operation moved by 1% of the time
where the time goes in v7:
time: 43.8 us; the launch traced here: 43.6 us
  Pallas kernels  43 us (98%)
  between operations  0.64 us (1%)
    pallas_call x1, Pallas kernels, per_device(): pl.pallas_call(body, out_shape=(flat, jax.ShapeDtypeStruct((ROOM, LAT), F...  41.5 us
    pallas_call x1, Pallas kernels, per_device(): pl.pallas_call(settle, out_shape=(flat, flat), in_specs=[vmem] * 3, out_s...  1.45 us

profile of v7, /device:TPU:1, one launch (start us, length us, event | category | flops | bytes accessed | tf_op | source)
XLA Modules:
  0.0 43.6 jit_solution(3830234639547555611)
XLA Ops:
  0.6 41.5 %wave_step.1 = (f32[1296,128]{1,0:T(8,128)S(1)}, f32[1312,128]{1,0:T(8,128)S(1)}, bf16[3,128,2,128]{3,2,1,0:T(2,128)(2,1)S(1)}) custom-call(f32[1296,128]{1,0:T(8,128)} %bitcast.8, f32[1296,128]{1,0:T(8,128)} %bitcast.9, s32[4,128]{1,0:T(4,128)} %refs_2_.1, f32[2,4,128]{2,1,0:T(4,128)} %refs_3_.1, s32[2,128]{1,0:T(2,128)} %bitcast.11, s32[1,128]{1,0:T(1,128)} %bitcast.12, ...), custom_call_target="tpu_custom_call" | custom-call | tf_op jit(solution)/shard_map/wave_step/pallas_call | solution.py:610
  42.2 1.4 %settle.1 = (f32[1296,128]{1,0:T(8,128)}, f32[1296,128]{1,0:T(8,128)}) custom-call(bf16[3,128,2,128]{3,2,1,0:T(2,128)(2,1)S(1)} %get-tuple-element.7.arrived, f32[1312,128]{1,0:T(8,128)S(1)} %get-tuple-element.8.nest, f32[1296,128]{1,0:T(8,128)S(1)} %get-tuple-element.9.g_next), custom_call_target="tpu_custom_call" | custom-call | tf_op jit(solution)/shard_map/settle/pallas_call | solution.py:691

commit v8 on v7

--- a/solution.py
+++ b/solution.py
@@ -401,9 +401,6 @@
         copy.start()
 
 
-    for copy in n_lon:
-        copy.start()
-
     chunk = 6
 
     def product(centre, upper, lower):
@@ -499,6 +496,8 @@
         pl.ds(FIRST_ROWS * LON, EAST - FIRST_ROWS, stride=LON), :
     ].astype(BF16)
     columns[1].start()
+    for copy in n_lon:
+        copy.start()
     pl.semaphore_wait(ring_sem, RING - 1)
     tell(half_sem, {"grid": x_peer})
 

time: 43.8 us -> 45 us (1.027)
  the two profiles are of different devices: /device:TPU:1 before, /device:TPU:8 now
where the time goes in v8:
time: 45 us; the launch traced here: 44.9 us
  Pallas kernels  44.2 us (98%)
  between operations  0.64 us (1%)
    pallas_call x1, Pallas kernels, per_device(): pl.pallas_call(body, out_shape=(flat, jax.ShapeDtypeStruct((ROOM, LAT), F...  42.8 us
    pallas_call x1, Pallas kernels, per_device(): pl.pallas_call(settle, out_shape=(flat, flat), in_specs=[vmem] * 3, out_s...  1.44 us

profile of v8, /device:TPU:8, one launch (start us, length us, event | category | flops | bytes accessed | tf_op | source)
XLA Modules:
  0.0 44.9 jit_solution(2695171532189548632)
XLA Ops:
  0.6 42.8 %wave_step.1 = (f32[1296,128]{1,0:T(8,128)S(1)}, f32[1312,128]{1,0:T(8,128)S(1)}, bf16[3,128,2,128]{3,2,1,0:T(2,128)(2,1)S(1)}) custom-call(f32[1296,128]{1,0:T(8,128)} %bitcast.8, f32[1296,128]{1,0:T(8,128)} %bitcast.9, s32[4,128]{1,0:T(4,128)} %refs_2_.1, f32[2,4,128]{2,1,0:T(4,128)} %refs_3_.1, s32[2,128]{1,0:T(2,128)} %bitcast.11, s32[1,128]{1,0:T(1,128)} %bitcast.12, ...), custom_call_target="tpu_custom_call" | custom-call | tf_op jit(solution)/shard_map/wave_step/pallas_call | solution.py:609
  43.4 1.4 %settle.1 = (f32[1296,128]{1,0:T(8,128)}, f32[1296,128]{1,0:T(8,128)}) custom-call(bf16[3,128,2,128]{3,2,1,0:T(2,128)(2,1)S(1)} %get-tuple-element.7.arrived, f32[1312,128]{1,0:T(8,128)S(1)} %get-tuple-element.8.nest, f32[1296,128]{1,0:T(8,128)S(1)} %get-tuple-element.9.g_next), custom_call_target="tpu_custom_call" | custom-call | tf_op jit(solution)/shard_map/settle/pallas_call | solution.py:690
